TPU v7x, 32 devices: a whole 2x2x4 slice. The times are simulated.
32 devices in a mesh: groups: 2 (over y), region: 4 (over z), head: 4 (over x, core).
Axes of the slice: x: 2, y: 2, z: 4, core: 2. Of those that a mesh axis runs over, the one named last changes fastest.
Arguments:
- video_queries: bfloat16 [2, 4, 256, 3072], P('groups', 'region', None, 'head'), parts along dimension 0, may hold values from -6 to 6
- video_keys: bfloat16 [2, 4, 256, 3072], P('groups', 'region', None, 'head'), parts along dimension 0, may hold values from -6 to 6
- video_values: bfloat16 [2, 4, 256, 3072], P('groups', 'region', None, 'head'), parts along dimension 0, may hold values from -12 to 12
- head_window: int32 [24, 2], P('head'), may hold values from 0 to 1
- prompt_keys: bfloat16 [512, 3072], P(('groups', 'region'), 'head'), parts along dimension 0, may hold values from -10 to 10
- prompt_values: bfloat16 [512, 3072], P(('groups', 'region'), 'head'), parts along dimension 0, may hold values from -10 to 10
- text_len: int32 [2], P('groups'), parts along dimension 0, may hold values from 64 to 256
Outputs:
- attended: bfloat16 [2, 4, 256, 3072], P('groups', 'region', None, 'head'), parts along dimension 0
There are 2 independent parts, one for each index of `groups`. A program takes and returns all parts, laid end to end along the dimension named above; an argument that names none is the same for every part. Nothing has to cross between parts.
Inputs may be any that keep to these rules, and one draw needn't show every extreme that they name: `head_window`: entry (h, 0) is head h's reach in tiles along grid rows, (h, 1) along grid columns; the window spans 2 r + 1 tiles along each. The first text_len[0] of the 256 prompt tokens are live.
All inputs are finite; a program needn't handle non-finite values.
Results may differ from a plain program's by a relative error of at most 0.0035.
Values may be sent and summed in bfloat16 or wider, within the bound.
A program may use at most 128 MiB of HBM per device.

v0:
```python
import functools
import math

import jax
import jax.numpy as jnp
from jax import lax
from jax.experimental import pallas as pl
from jax.experimental.pallas import tpu as pltpu
from jax.sharding import PartitionSpec as P

MESH = pl.DeviceIdType.MESH
MASKED = -1e30
VMEM_BUDGET = 24 * 2**20


def absorb(softmax_state, query_heads, block_keys, block_values, allowed):
    running_max, running_sum, weighted = softmax_state
    score_scale = 1.0 / math.sqrt(query_heads.shape[-1])
    scores = (
        jnp.einsum("sqhd,skhd->shqk", query_heads, block_keys, preferred_element_type=jnp.float32)
        * score_scale
    )
    scores = jnp.where(allowed, scores, -jnp.inf)
    new_max = jnp.maximum(running_max, jnp.max(scores, axis=-1, keepdims=True))
    weights = jnp.exp(scores - new_max)
    rescale = jnp.exp(running_max - new_max)
    running_sum = running_sum * rescale + jnp.sum(weights, axis=-1, keepdims=True)
    contribution = jnp.einsum(
        "shqk,skhd->sqhd",
        weights.astype(jnp.bfloat16),
        block_values,
        preferred_element_type=jnp.float32,
    )
    weighted = weighted * jnp.transpose(rescale, (0, 2, 1, 3)) + contribution
    return (new_max, running_sum, weighted)


def gathered(
    video_queries, video_keys, video_values, head_window, prompt_keys, prompt_values, text_len
):
    slab_count = video_queries.shape[0]
    tile_tok = video_queries.shape[2]
    features = video_queries.shape[3]
    head_count = head_window.shape[0]
    head_dim = features // head_count
    region_count = lax.axis_size("region")
    grid_cols = min(8, region_count // 2)
    position = lax.axis_index("region")
    my_row = position // grid_cols
    my_col = position % grid_cols
    reach_rows = head_window[:, 0]
    reach_cols = head_window[:, 1]
    query_heads = video_queries.reshape(slab_count, tile_tok, head_count, head_dim)
    paired = jnp.stack([video_keys, video_values])
    stat_shape = (slab_count, head_count, tile_tok, 1)
    softmax_state = (
        jnp.full(stat_shape, -1e30, jnp.float32),
        jnp.zeros(stat_shape, jnp.float32),
        jnp.zeros((slab_count, tile_tok, head_count, head_dim), jnp.float32),
    )
    shard_piece = lax.all_gather(paired, "region", axis=2, tiled=True)
    piece_count = shard_piece.shape[2]

    def one_tile(tile_slot, state_in):
        row_step = tile_slot // grid_cols - my_row
        col_step = tile_slot % grid_cols - my_col
        within = (jnp.abs(row_step) <= reach_rows) & (jnp.abs(col_step) <= reach_cols)
        tile_pair = lax.dynamic_slice_in_dim(shard_piece, tile_slot, 1, 2)
        block_keys = tile_pair[0].reshape(slab_count, tile_tok, head_count, head_dim)
        block_values = tile_pair[1].reshape(slab_count, tile_tok, head_count, head_dim)
        allowed = within.reshape(1, head_count, 1, 1)

        def take_tile(state_keep):
            return absorb(state_keep, query_heads, block_keys, block_values, allowed)

        def keep_state(state_keep):
            return state_keep

        return lax.cond(jnp.any(within), take_tile, keep_state, state_in)

    softmax_state = lax.fori_loop(0, piece_count, one_tile, softmax_state)
    live_text = text_len[0]
    prompt_piece = (
        lax.all_gather(prompt_keys, "region", axis=0, tiled=True),
        lax.all_gather(prompt_values, "region", axis=0, tiled=True),
    )
    piece_count = prompt_piece[0].shape[0]
    block_keys = prompt_piece[0].reshape(1, piece_count, head_count, head_dim)
    block_values = prompt_piece[1].reshape(1, piece_count, head_count, head_dim)
    allowed = (jnp.arange(piece_count, dtype=jnp.int32) < live_text).reshape(1, 1, 1, piece_count)
    softmax_state = absorb(softmax_state, query_heads, block_keys, block_values, allowed)
    running_max, running_sum, weighted = softmax_state
    result = weighted / jnp.transpose(running_sum, (0, 2, 1, 3))
    return result.reshape(slab_count, 1, tile_tok, features).astype(jnp.bfloat16)


def attend(queries, blocks, score_scale):
    scores = [
        lax.dot_general(
            queries, keys, (((1,), (1,)), ((), ())), preferred_element_type=jnp.float32
        )
        + bias
        for keys, _, bias in blocks
    ]
    row_max = jnp.max(functools.reduce(jnp.maximum, scores), axis=-1, keepdims=True)
    weights = [jnp.exp2((block - row_max) * (score_scale / math.log(2.0))) for block in scores]
    row_sum = jnp.sum(functools.reduce(jnp.add, weights), axis=-1, keepdims=True)
    weighted = functools.reduce(
        jnp.add,
        [
            jnp.dot(weight.astype(jnp.bfloat16), values, preferred_element_type=jnp.float32)
            for weight, (_, values, _) in zip(weights, blocks)
        ],
    )
    return (weighted * (1.0 / row_sum)).astype(jnp.bfloat16)

def exchange_kernel(
    dims,
    window_ref, text_len_ref, q_ref, k_ref, v_ref, tk_ref, tv_ref, o_fin, x_fin,
    k_own, tk_own, v_own, tv_own, q_own, o_own,
    k_ext, tk_ext, v_ext, tv_ext, q_ext, o_ext,
    own_send, own_recv, o_send, o_recv,
    ext_send, ext_recv, x_send, x_recv, local_sem,
):
    n, heads, head_dim, grid_cols = dims
    me = lax.axis_index("region")
    odd = lax.axis_index("head") % 2
    per_device = heads // n
    extra = heads - per_device * n
    width = per_device * head_dim
    half = n // 2
    side, place = me // half, me % half
    score_scale = 1.0 / math.sqrt(head_dim)
    peers = [(1 - side) * half + lax.rem(place + j, half) for j in range(half)]
    peers += [side * half + lax.rem(place + j, half) for j in range(1, half)]

    def peer_at(j):
        across = j < half
        there = jnp.where(across, 1 - side, side)
        return there * half + lax.rem(place + jnp.where(across, j, j - half + 1), half)

    barrier = pltpu.get_barrier_semaphore()
    for peer in peers:
        pl.semaphore_signal(barrier, inc=1, device_id={"region": peer}, device_id_type=MESH)

    def extra_owner(e):
        return jnp.where(odd == 0, e, n - 1 - e)

    my_extra = jnp.where(odd == 0, me, n - 1 - me)
    inputs = (k_ref, tk_ref, v_ref, tv_ref, q_ref)
    own_bufs = (k_own, tk_own, v_own, tv_own, q_own)
    ext_bufs = (k_ext, tk_ext, v_ext, tv_ext, q_ext)
    parts, key_parts, query_part = range(5), range(4), 4

    def own_cols(owner):
        return pl.ds(pl.multiple_of(owner * width, head_dim), width)

    def ext_cols(e):
        return pl.ds(pl.multiple_of(n * width + e * head_dim, head_dim), head_dim)

    def fin_cols(e):
        return pl.ds(pl.multiple_of(e * head_dim, head_dim), head_dim)

    def remote(src, dst, send_sem, recv_sem, target):
        return pltpu.make_async_remote_copy(
            src_ref=src,
            dst_ref=dst,
            send_sem=send_sem,
            recv_sem=recv_sem,
            device_id={"region": target},
            device_id_type=MESH,
        )

    def own_copy(target, source, j, i):
        return remote(
            inputs[i].at[:, own_cols(target)],
            own_bufs[i].at[source],
            own_send.at[j, i],
            own_recv.at[source, i],
            target,
        )

    def ext_copy(e, target, source, i):
        return remote(
            inputs[i].at[:, ext_cols(e)],
            ext_bufs[i].at[source],
            ext_send.at[e, i],
            ext_recv.at[source, i],
            target,
        )

    def o_copy(target, source, j):
        return remote(
            o_own.at[target],
            o_fin.at[:, own_cols(source)],
            o_send.at[j],
            o_recv.at[source],
            target,
        )

    def x_copy(e, target, j):
        return remote(
            o_ext.at[target], x_fin.at[:, fin_cols(e)], x_send.at[j], x_recv.at[e], target
        )

    local = [
        pltpu.make_async_copy(inputs[i].at[:, own_cols(me)], own_bufs[i].at[me], local_sem.at[i])
        for i in parts
    ]
    for copy in local:
        copy.start()
    local_ext = []
    if extra:
        local_ext = [
            pltpu.make_async_copy(
                inputs[i].at[:, ext_cols(lax.rem(my_extra, extra))],
                ext_bufs[i].at[me],
                local_sem.at[5 + i],
            )
            for i in parts
        ]
        for copy in local_ext:
            copy.start()

    pl.semaphore_wait(barrier, n - 1)
    for j, peer in enumerate(peers):
        for i in key_parts:
            own_copy(peer, me, j, i).start()
    for j, peer in enumerate(peers):
        own_copy(peer, me, j, query_part).start()

    for pieces in (key_parts, (query_part,)):
        for e in range(extra):

            @pl.when(me != extra_owner(e))
            def _(e=e, pieces=pieces):
                for i in pieces:
                    ext_copy(e, extra_owner(e), me, i).start()


    text_bias = jnp.where(
        lax.broadcasted_iota(jnp.int32, (1, n * tk_ref.shape[0]), 1) < text_len_ref[0], 0.0, MASKED
    )

    def tile_bias(head, tile_q, tile_k):
        rows = jnp.abs(tile_q // grid_cols - tile_k // grid_cols)
        cols = jnp.abs(tile_q % grid_cols - tile_k % grid_cols)
        within = (rows <= window_ref[0, head]) & (cols <= window_ref[1, head])
        return jnp.where(within, 0.0, MASKED)

    def tile_attend(bufs, slot, head, tile):
        keys, text_keys, values, text_values, queries = bufs
        lanes = pl.ds(slot * head_dim, head_dim)
        blocks = [(keys[t, :, lanes], values[t, :, lanes], tile_bias(head, tile, t)) for t in range(n)]
        blocks.append(
            (
                text_keys[:, :, lanes].reshape(-1, head_dim),
                text_values[:, :, lanes].reshape(-1, head_dim),
                text_bias,
            )
        )
        return attend(queries[tile, :, lanes], blocks, score_scale)

    for copy in local + local_ext:
        copy.wait()
    def own_tile(out, tile):
        for slot in range(per_device):
            out[:, pl.ds(slot * head_dim, head_dim)] = tile_attend(
                own_bufs, slot, me * per_device + slot, tile
            )

    for peer in peers:
        for i in key_parts:
            own_copy(me, peer, 0, i).wait_recv()

    def own_step(j, _):
        peer = peer_at(j)

        @pl.when(j < n - 1)
        def _():
            own_copy(me, peer, 0, query_part).wait_recv()

        own_tile(o_own.at[peer], peer)

        @pl.when(j < n - 1)
        def _():
            o_copy(peer, me, j).start()

        return 0

    lax.fori_loop(0, n, own_step, 0)

    if extra:

        @pl.when(my_extra < extra)
        def _():
            head = n * per_device + my_extra
            for peer in peers:
                for i in key_parts:
                    ext_copy(my_extra, me, peer, i).wait_recv()

            def ext_step(j, _):
                peer = peer_at(j)

                @pl.when(j < n - 1)
                def _():
                    ext_copy(my_extra, me, peer, query_part).wait_recv()

                o_ext[peer] = tile_attend(ext_bufs, 0, head, peer)

                @pl.when(j < n - 1)
                def _():
                    x_copy(my_extra, peer, j).start()

                return 0

            lax.fori_loop(0, n, ext_step, 0)
            x_fin[:, fin_cols(my_extra)] = o_ext[me]

    for e in range(extra):

        @pl.when(me != extra_owner(e))
        def _(e=e):
            x_copy(e, me, 0).wait_recv()

    for peer in peers:
        o_copy(me, peer, 0).wait_recv()
    o_fin[:, own_cols(me)] = o_own[me]

    for j, peer in enumerate(peers):
        for i in parts:
            own_copy(peer, me, j, i).wait_send()
        o_copy(peer, me, j).wait_send()
    for e in range(extra):

        @pl.when(me != extra_owner(e))
        def _(e=e):
            for i in parts:
                ext_copy(e, extra_owner(e), me, i).wait_send()

    if extra:

        @pl.when(my_extra < extra)
        def _():
            for j, peer in enumerate(peers):
                x_copy(my_extra, peer, j).wait_send()


def assemble_kernel(own_ref, ext_ref, out_ref, sems):
    split, features = own_ref.shape[1], out_ref.shape[1]
    copies = [pltpu.make_async_copy(own_ref, out_ref.at[:, pl.ds(0, split)], sems.at[0])]
    if features > split:
        rest = pl.ds(split, features - split)
        copies.append(pltpu.make_async_copy(ext_ref, out_ref.at[:, rest], sems.at[1]))
    for copy in copies:
        copy.start()
    for copy in copies:
        copy.wait()


def exchange(
    video_queries, video_keys, video_values, head_window, prompt_keys, prompt_values, text_len
):
    n = lax.axis_size("region")
    tile_tok, features = video_queries.shape[2:]
    text_tok = prompt_keys.shape[0]
    heads = head_window.shape[0]
    head_dim = features // heads
    width = heads // n * head_dim
    extra = max(heads % n, 1)
    grid_cols = min(8, n // 2)
    kind = video_queries.dtype
    any_spec = pl.BlockSpec(memory_space=pl.ANY)
    smem_spec = pl.BlockSpec(memory_space=pltpu.SMEM)
    tile_own = pltpu.VMEM((n, tile_tok, width), kind)
    text_own = pltpu.VMEM((n, text_tok, width), kind)
    tile_ext = pltpu.VMEM((n, tile_tok, head_dim), kind)
    text_ext = pltpu.VMEM((n, text_tok, head_dim), kind)
    dma = pltpu.SemaphoreType.DMA
    keys_total = n * (tile_tok + text_tok)
    landed = pl.pallas_call(
        functools.partial(exchange_kernel, (n, heads, head_dim, grid_cols)),
        out_shape=(
            pltpu.VMEM((tile_tok, n * width), kind),
            pltpu.VMEM((tile_tok, extra * head_dim), kind),
        ),
        in_specs=[smem_spec, smem_spec] + [any_spec] * 5,
        out_specs=[pl.BlockSpec(memory_space=pltpu.VMEM)] * 2,
        scratch_shapes=[
            tile_own, text_own, tile_own, text_own, tile_own, tile_own,
            tile_ext, text_ext, tile_ext, text_ext, tile_ext, tile_ext,
            dma((n, 5)), dma((n, 5)), dma((n,)), dma((n,)),
            dma((extra, 5)), dma((n, 5)), dma((n,)), dma((extra,)), dma((10,)),
        ],
        compiler_params=pltpu.CompilerParams(collective_id=0, has_side_effects=True),
        cost_estimate=pl.CostEstimate(
            flops=4 * tile_tok * features * keys_total,
            bytes_accessed=8 * tile_tok * features * n,
            transcendentals=tile_tok * heads * keys_total,
        ),
        name="exchange_attend",
    )(
        head_window.T,
        text_len,
        video_queries.reshape(tile_tok, features),
        video_keys.reshape(tile_tok, features),
        video_values.reshape(tile_tok, features),
        prompt_keys,
        prompt_values,
    )
    result = pl.pallas_call(
        assemble_kernel,
        out_shape=jax.ShapeDtypeStruct((tile_tok, features), kind),
        in_specs=[pl.BlockSpec(memory_space=pltpu.VMEM)] * 2,
        out_specs=any_spec,
        scratch_shapes=[dma((2,))],
        name="assemble",
    )(*[pltpu.with_memory_space_constraint(piece, pltpu.VMEM) for piece in landed])
    return result.reshape(video_queries.shape)


def fits(video_queries, head_window):
    n = lax.axis_size("region")
    heads = head_window.shape[0]
    slabs, tiles, tile_tok, features = video_queries.shape
    landed = 12 * n * tile_tok * features
    return (
        slabs == 1 and tiles == 1 and n % 2 == 0 and heads >= n
        and features // heads == 128 and landed < VMEM_BUDGET
    )


def shards(
    video_queries, video_keys, video_values, head_window, prompt_keys, prompt_values, text_len
):
    route = exchange if fits(video_queries, head_window) else gathered
    return route(
        video_queries, video_keys, video_values, head_window, prompt_keys, prompt_values, text_len
    )


def solution(mesh):
    in_specs = (
        P("groups", "region", None, "head"),
        P("groups", "region", None, "head"),
        P("groups", "region", None, "head"),
        P("head", None),
        P(("groups", "region"), "head"),
        P(("groups", "region"), "head"),
        P("groups"),
    )
    out_specs = P("groups", "region", None, "head")
    return jax.shard_map(shards, mesh=mesh, in_specs=in_specs, out_specs=out_specs, check_vma=False)
```

profile of v0, /device:TPU:0, one launch (start us, length us, event | category | flops | bytes accessed | tf_op | source)
XLA Modules:
  0.0 48.2 jit_solution(16982340339730082771)
XLA Ops:
  0.7 46.7 %exchange_attend.1 = (bf16[256,512]{1,0:T(8,128)(2,1)S(1)}, bf16[256,256]{1,0:T(8,128)(2,1)S(1)}) custom-call(s32[2,6]{1,0:T(2,128)} %bitcast.8, s32[1]{0:T(128)S(6)} %copy.8.text_len_ref, bf16[256,768]{1,0:T(8,128)(2,1)} %bitcast.5, bf16[256,768]{1,0:T(8,128)(2,1)} %bitcast.6, bf16[256,768]{1,0:T(8,128)(2,1)} %bitcast.7, bf16[64,768]{1,0:T(8,128)(2,1)} %tk_ref.1, ...), custom_call_target="tpu_custom_call" | custom-call | flops 1006632960 | bytes 6291456 | tf_op jit(solution)/shard_map/exchange_attend/pallas_call | solution.py:381
  47.4 0.8 %assemble.1 = bf16[256,768]{1,0:T(8,128)(2,1)} custom-call(bf16[256,512]{1,0:T(8,128)(2,1)S(1)} %get-tuple-element.7.own_ref, bf16[256,256]{1,0:T(8,128)(2,1)S(1)} %get-tuple-element.8.ext_ref), custom_call_target="tpu_custom_call" | custom-call | tf_op jit(solution)/shard_map/assemble/pallas_call | solution.py:411
where the time goes:
time: 48.3 us; the launch traced here: 48.2 us
  Pallas kernels  47.5 us (98%)
  between operations  0.66 us (1%)
    pallas_call x1, Pallas kernels, exchange(): pl.pallas_call(functools.partial(exchange_kernel, (n, heads, head_dim, gr...  46.7 us

commit v1 on v0

v1 whole, which is shorter than its diff:
```python
import functools
import math

import jax
import jax.numpy as jnp
from jax import lax
from jax.experimental import pallas as pl
from jax.experimental.pallas import tpu as pltpu
from jax.sharding import PartitionSpec as P

MESH = pl.DeviceIdType.MESH
MASKED = -1e30
FLOOR = -1e20
TINY = 1e-30
VMEM_BUDGET = 24 * 2**20


def absorb(softmax_state, query_heads, block_keys, block_values, allowed):
    running_max, running_sum, weighted = softmax_state
    score_scale = 1.0 / math.sqrt(query_heads.shape[-1])
    scores = (
        jnp.einsum("sqhd,skhd->shqk", query_heads, block_keys, preferred_element_type=jnp.float32)
        * score_scale
    )
    scores = jnp.where(allowed, scores, -jnp.inf)
    new_max = jnp.maximum(running_max, jnp.max(scores, axis=-1, keepdims=True))
    weights = jnp.exp(scores - new_max)
    rescale = jnp.exp(running_max - new_max)
    running_sum = running_sum * rescale + jnp.sum(weights, axis=-1, keepdims=True)
    contribution = jnp.einsum(
        "shqk,skhd->sqhd",
        weights.astype(jnp.bfloat16),
        block_values,
        preferred_element_type=jnp.float32,
    )
    weighted = weighted * jnp.transpose(rescale, (0, 2, 1, 3)) + contribution
    return (new_max, running_sum, weighted)


def gathered(
    video_queries, video_keys, video_values, head_window, prompt_keys, prompt_values, text_len
):
    slab_count = video_queries.shape[0]
    tile_tok = video_queries.shape[2]
    features = video_queries.shape[3]
    head_count = head_window.shape[0]
    head_dim = features // head_count
    region_count = lax.axis_size("region")
    grid_cols = min(8, region_count // 2)
    position = lax.axis_index("region")
    my_row = position // grid_cols
    my_col = position % grid_cols
    reach_rows = head_window[:, 0]
    reach_cols = head_window[:, 1]
    query_heads = video_queries.reshape(slab_count, tile_tok, head_count, head_dim)
    paired = jnp.stack([video_keys, video_values])
    stat_shape = (slab_count, head_count, tile_tok, 1)
    softmax_state = (
        jnp.full(stat_shape, -1e30, jnp.float32),
        jnp.zeros(stat_shape, jnp.float32),
        jnp.zeros((slab_count, tile_tok, head_count, head_dim), jnp.float32),
    )
    shard_piece = lax.all_gather(paired, "region", axis=2, tiled=True)
    piece_count = shard_piece.shape[2]

    def one_tile(tile_slot, state_in):
        row_step = tile_slot // grid_cols - my_row
        col_step = tile_slot % grid_cols - my_col
        within = (jnp.abs(row_step) <= reach_rows) & (jnp.abs(col_step) <= reach_cols)
        tile_pair = lax.dynamic_slice_in_dim(shard_piece, tile_slot, 1, 2)
        block_keys = tile_pair[0].reshape(slab_count, tile_tok, head_count, head_dim)
        block_values = tile_pair[1].reshape(slab_count, tile_tok, head_count, head_dim)
        allowed = within.reshape(1, head_count, 1, 1)

        def take_tile(state_keep):
            return absorb(state_keep, query_heads, block_keys, block_values, allowed)

        def keep_state(state_keep):
            return state_keep

        return lax.cond(jnp.any(within), take_tile, keep_state, state_in)

    softmax_state = lax.fori_loop(0, piece_count, one_tile, softmax_state)
    live_text = text_len[0]
    prompt_piece = (
        lax.all_gather(prompt_keys, "region", axis=0, tiled=True),
        lax.all_gather(prompt_values, "region", axis=0, tiled=True),
    )
    piece_count = prompt_piece[0].shape[0]
    block_keys = prompt_piece[0].reshape(1, piece_count, head_count, head_dim)
    block_values = prompt_piece[1].reshape(1, piece_count, head_count, head_dim)
    allowed = (jnp.arange(piece_count, dtype=jnp.int32) < live_text).reshape(1, 1, 1, piece_count)
    softmax_state = absorb(softmax_state, query_heads, block_keys, block_values, allowed)
    running_max, running_sum, weighted = softmax_state
    result = weighted / jnp.transpose(running_sum, (0, 2, 1, 3))
    return result.reshape(slab_count, 1, tile_tok, features).astype(jnp.bfloat16)


def partial_attend(keys, values_t, queries, biases, text_bias, log2_scale):
    tile_tok = queries.shape[0]
    scores = lax.dot_general(
        keys, queries, (((1,), (1,)), ((), ())), preferred_element_type=jnp.float32
    )
    blocks = [scores[i * tile_tok : (i + 1) * tile_tok] for i in range(len(biases))]
    text = scores[len(biases) * tile_tok :] + text_bias
    row_max = jnp.max(text, axis=0, keepdims=True)
    for block, bias in zip(blocks, biases):
        row_max = jnp.maximum(row_max, jnp.max(block, axis=0, keepdims=True) + bias)
    row_max = jnp.maximum(row_max, FLOOR)
    weights = [
        jnp.exp2(block * log2_scale + (bias - row_max) * log2_scale)
        for block, bias in zip(blocks, biases)
    ]
    weights.append(jnp.exp2(text * log2_scale - row_max * log2_scale))
    row_sum = functools.reduce(
        jnp.add, [jnp.sum(weight, axis=0, keepdims=True) for weight in weights]
    )
    rounded = jnp.concatenate([weight.astype(jnp.bfloat16) for weight in weights], axis=0)
    weighted = jnp.dot(values_t, rounded, preferred_element_type=jnp.float32)
    return row_max * log2_scale, jnp.maximum(row_sum, TINY), weighted


def pair_kernel(
    dims,
    window_ref, text_len_ref, q_ref, k_ref, v_ref, tk_ref, tv_ref, out_ref,
    keys, values, q_own, q_near, q_far, o_out, o_in, e_out, e_in, held, stats, text_bias,
    kv_send, kv_recv, near_send, near_recv, far_send, far_recv, pass_send,
    o_send, o_recv, e_send, e_recv, local_sem,
):
    n, heads, head_dim, grid_cols = dims
    tile_tok, text_tok = q_ref.shape[0], tk_ref.shape[0]
    half = n // 2
    me = lax.axis_index("region")
    side, place = me // half, me % half
    near = side * half + (half - 1 - place)
    inner = side + place == half - 1
    opposite = n - 1 - me
    across = lax.rem(me + half, n)
    log2_scale = 1.0 / (math.sqrt(head_dim) * math.log(2.0))

    barrier = pltpu.get_barrier_semaphore()

    def greet(target):
        pl.semaphore_signal(barrier, inc=1, device_id={"region": target}, device_id_type=MESH)

    def lanes(h):
        return pl.ds(pl.multiple_of(h * head_dim, head_dim), head_dim)

    def remote(src, dst, send_sem, recv_sem, target):
        return pltpu.make_async_remote_copy(
            src_ref=src,
            dst_ref=dst,
            send_sem=send_sem,
            recv_sem=recv_sem,
            device_id={"region": target},
            device_id_type=MESH,
        )

    sources = (k_ref, tk_ref, v_ref, tv_ref)
    buffers = (keys, keys, values, values)
    starts = (0, 2 * tile_tok, 0, 2 * tile_tok)
    lengths = (tile_tok, text_tok, tile_tok, text_tok)
    parts = range(4)

    def kv_copy(h, i):
        return remote(
            sources[i].at[:, lanes(h)],
            buffers[i].at[pl.ds(starts[i] + lengths[i], lengths[i]), lanes(h)],
            kv_send.at[h, i],
            kv_recv.at[h, i],
            near,
        )

    def near_copy(h):
        return remote(q_ref.at[:, lanes(h)], q_near.at[h], near_send.at[h], near_recv.at[h], near)

    def far_copy(h):
        return remote(
            q_ref.at[:, lanes(h)], q_far.at[h, 0], far_send.at[h], far_recv.at[h, 0], opposite
        )

    def pass_copy(h):
        return remote(
            q_near.at[h], q_far.at[h, 1], pass_send.at[h], far_recv.at[h, 1], opposite
        )

    def o_copy(h, j, target):
        return remote(o_out.at[h, j], o_in.at[h], o_send.at[h, j], o_recv.at[h], target)

    def e_copy(h, j, target):
        return remote(e_out.at[h, j], e_in.at[h], e_send.at[h, j], e_recv.at[h], target)

    local = [
        pltpu.make_async_copy(
            sources[i], buffers[i].at[pl.ds(starts[i], lengths[i]), :], local_sem.at[i]
        )
        for i in parts
    ]
    local.append(pltpu.make_async_copy(q_ref, q_own, local_sem.at[4]))

    def each_head(step):
        def body(h, carry):
            step(h)
            return carry

        lax.fori_loop(0, heads, body, 0)

    greet(near)

    @pl.when(inner)
    def _():
        greet(opposite)

    for copy in local:
        copy.start()

    @pl.when(inner)
    def _():
        pl.semaphore_wait(barrier, 2)
        for h in range(heads):
            far_copy(h).start()

    @pl.when(jnp.logical_not(inner))
    def _():
        pl.semaphore_wait(barrier, 1)
        for h in range(heads):
            near_copy(h).start()

    for h in range(heads):
        for i in parts:
            kv_copy(h, i).start()

    index = lax.broadcasted_iota(jnp.int32, text_bias.shape, 0)
    index = index + jnp.where(index < text_tok, me * text_tok, (near - 1) * text_tok)
    text_bias[...] = jnp.where(index < text_len_ref[0], 0.0, MASKED)

    def tile_bias(head, tile_q, tile_k):
        rows = jnp.abs(tile_q // grid_cols - tile_k // grid_cols)
        cols = jnp.abs(tile_q % grid_cols - tile_k % grid_cols)
        within = (rows <= window_ref[0, head]) & (cols <= window_ref[1, head])
        return jnp.where(within, 0.0, MASKED)

    def attend(h, keys_h, values_t, queries, tile):
        biases = (tile_bias(h, tile, me), tile_bias(h, tile, near))
        return partial_attend(keys_h, values_t, queries, biases, text_bias[...], log2_scale)

    def hold(h, keys_h, values_t):
        row_max, row_sum, weighted = attend(h, keys_h, values_t, q_own[:, lanes(h)], me)
        held[h] = weighted
        stats[h, 0:1, :] = row_max
        stats[h, 1:2, :] = row_sum

    def take_kv(h):
        for i in parts:
            kv_copy(h, i).wait_recv()
        return keys[:, lanes(h)], values[:, lanes(h)].T

    for copy in local:
        copy.wait()

    @pl.when(inner)
    def _():
        for h in range(heads):
            near_copy(h).wait_recv()
            pass_copy(h).start()

        def step(h):
            keys_h, values_t = take_kv(h)
            for j, tile in ((1, across), (0, opposite)):
                far_recv_copy = pass_copy(h) if j else far_copy(h)
                far_recv_copy.wait_recv()
                row_max, row_sum, weighted = attend(h, keys_h, values_t, q_far[h, j], tile)
                o_out[h, j] = (weighted * (1.0 / row_sum)).astype(o_out.dtype)
                e_out[h, j] = row_max + jnp.log(row_sum) * (1.0 / math.log(2.0))
                o_copy(h, j, tile).start()
                e_copy(h, j, tile).start()
            hold(h, keys_h, values_t)

        each_head(step)

    @pl.when(jnp.logical_not(inner))
    def _():
        def step(h):
            hold(h, *take_kv(h))

        each_head(step)

    def finish(h):
        o_copy(h, 0, across).wait_recv()
        e_copy(h, 0, across).wait_recv()
        own_max, own_sum, far_max = stats[h, 0:1, :], stats[h, 1:2, :], e_in[h]
        top = jnp.maximum(own_max, far_max)
        own_part, far_part = jnp.exp2(own_max - top), jnp.exp2(far_max - top)
        inverse = 1.0 / (own_sum * own_part + far_part)
        result = held[h] * (own_part * inverse)
        result = result + o_in[h].astype(jnp.float32) * (far_part * inverse)
        out_ref[:, lanes(h)] = result.T.astype(out_ref.dtype)

    each_head(finish)

    def sent(h):
        for i in parts:
            kv_copy(h, i).wait_send()

    each_head(sent)

    @pl.when(inner)
    def _():
        def done(h):
            far_copy(h).wait_send()
            pass_copy(h).wait_send()
            for j in range(2):
                o_copy(h, j, across).wait_send()
                e_copy(h, j, across).wait_send()

        each_head(done)

    @pl.when(jnp.logical_not(inner))
    def _():
        def done(h):
            near_copy(h).wait_send()

        each_head(done)


def assemble_kernel(own_ref, out_ref, sem):
    copy = pltpu.make_async_copy(own_ref, out_ref, sem)
    copy.start()
    copy.wait()


def paired(
    video_queries, video_keys, video_values, head_window, prompt_keys, prompt_values, text_len
):
    n = lax.axis_size("region")
    tile_tok, features = video_queries.shape[2:]
    text_tok = prompt_keys.shape[0]
    heads = head_window.shape[0]
    head_dim = features // heads
    grid_cols = min(8, n // 2)
    kind = video_queries.dtype
    any_spec = pl.BlockSpec(memory_space=pl.ANY)
    smem_spec = pl.BlockSpec(memory_space=pltpu.SMEM)
    key_rows = 2 * (tile_tok + text_tok)
    wide, tall = (tile_tok, head_dim), (head_dim, tile_tok)
    dma = pltpu.SemaphoreType.DMA
    landed = pl.pallas_call(
        functools.partial(pair_kernel, (n, heads, head_dim, grid_cols)),
        out_shape=pltpu.VMEM((tile_tok, features), kind),
        in_specs=[smem_spec, smem_spec] + [any_spec] * 5,
        out_specs=pl.BlockSpec(memory_space=pltpu.VMEM),
        scratch_shapes=[
            pltpu.VMEM((key_rows, features), kind),
            pltpu.VMEM((key_rows, features), kind),
            pltpu.VMEM((tile_tok, features), kind),
            pltpu.VMEM((heads,) + wide, kind),
            pltpu.VMEM((heads, 2) + wide, kind),
            pltpu.VMEM((heads, 2) + tall, kind),
            pltpu.VMEM((heads,) + tall, kind),
            pltpu.VMEM((heads, 2, 1, tile_tok), jnp.float32),
            pltpu.VMEM((heads, 1, tile_tok), jnp.float32),
            pltpu.VMEM((heads,) + tall, jnp.float32),
            pltpu.VMEM((heads, 2, tile_tok), jnp.float32),
            pltpu.VMEM((2 * text_tok, tile_tok), jnp.float32),
            dma((heads, 4)), dma((heads, 4)), dma((heads,)), dma((heads,)),
            dma((heads,)), dma((heads, 2)), dma((heads,)),
            dma((heads, 2)), dma((heads,)), dma((heads, 2)), dma((heads,)), dma((5,)),
        ],
        compiler_params=pltpu.CompilerParams(collective_id=0, has_side_effects=True),
        cost_estimate=pl.CostEstimate(
            flops=12 * tile_tok * features * key_rows,
            bytes_accessed=8 * tile_tok * features * n,
            transcendentals=3 * tile_tok * heads * key_rows,
        ),
        name="pair_attend",
    )(
        head_window.T,
        text_len,
        video_queries.reshape(tile_tok, features),
        video_keys.reshape(tile_tok, features),
        video_values.reshape(tile_tok, features),
        prompt_keys,
        prompt_values,
    )
    result = pl.pallas_call(
        assemble_kernel,
        out_shape=jax.ShapeDtypeStruct((tile_tok, features), kind),
        in_specs=[pl.BlockSpec(memory_space=pltpu.VMEM)],
        out_specs=any_spec,
        scratch_shapes=[dma],
        name="assemble",
    )(pltpu.with_memory_space_constraint(landed, pltpu.VMEM))
    return result.reshape(video_queries.shape)


def fits(video_queries, head_window, prompt_keys):
    n = lax.axis_size("region")
    heads = head_window.shape[0]
    slabs, tiles, tile_tok, features = video_queries.shape
    landed = 32 * tile_tok * features
    return (
        slabs == 1 and tiles == 1 and n // 2 == 2 and n % 2 == 0
        and features == 128 * heads and tile_tok % 128 == 0
        and prompt_keys.shape[0] % 16 == 0 and landed < VMEM_BUDGET
    )


def shards(
    video_queries, video_keys, video_values, head_window, prompt_keys, prompt_values, text_len
):
    route = paired if fits(video_queries, head_window, prompt_keys) else gathered
    return route(
        video_queries, video_keys, video_values, head_window, prompt_keys, prompt_values, text_len
    )


def solution(mesh):
    in_specs = (
        P("groups", "region", None, "head"),
        P("groups", "region", None, "head"),
        P("groups", "region", None, "head"),
        P("head", None),
        P(("groups", "region"), "head"),
        P(("groups", "region"), "head"),
        P("groups"),
    )
    out_specs = P("groups", "region", None, "head")
    return jax.shard_map(shards, mesh=mesh, in_specs=in_specs, out_specs=out_specs, check_vma=False)
```

time: 48.3 us -> 43.4 us (0.90)
  Pallas kernels: 47.5 us -> 42.5 us
    pallas_call x2, Pallas kernels: 47.5 us -> 42.5 us  [the longest x1 41.8 us: paired(): pl.pallas_call(functools.partial(pair_kernel, (n, heads, head_dim, grid_c...]
where the time goes in v1:
time: 43.4 us; the launch traced here: 43.2 us
  Pallas kernels  42.5 us (98%)
  between operations  0.66 us (2%)
    pallas_call x1, Pallas kernels, paired(): pl.pallas_call(functools.partial(pair_kernel, (n, heads, head_dim, grid_c...  41.8 us

profile of v1, /device:TPU:0, one launch (start us, length us, event | category | flops | bytes accessed | tf_op | source)
XLA Modules:
  0.0 43.2 jit_solution(8923675007188372584)
XLA Ops:
  0.7 41.8 %pair_attend.1.own_ref = bf16[256,768]{1,0:T(8,128)(2,1)S(1)} custom-call(s32[2,6]{1,0:T(2,128)} %bitcast.8, s32[1]{0:T(128)S(6)} %copy.8.text_len_ref, bf16[256,768]{1,0:T(8,128)(2,1)} %bitcast.5, bf16[256,768]{1,0:T(8,128)(2,1)} %bitcast.6, bf16[256,768]{1,0:T(8,128)(2,1)} %bitcast.7, bf16[64,768]{1,0:T(8,128)(2,1)} %tk_ref.1, bf16[64,768]{1,0:T(8,128)(2,1)} %tv_ref.1), custom_call_target="tpu_custom_call" | custom-call | flops 1509949440 | bytes 6291456 | tf_op jit(solution)/shard_map/pair_attend/pallas_call | solution.py:347
  42.4 0.8 %assemble.1 = bf16[256,768]{1,0:T(8,128)(2,1)} custom-call(bf16[256,768]{1,0:T(8,128)(2,1)S(1)} %pair_attend.1.own_ref), custom_call_target="tpu_custom_call" | custom-call | tf_op jit(solution)/shard_map/assemble/pallas_call | solution.py:385

commit v2 on v1

--- a/solution.py
+++ b/solution.py
@@ -122,8 +122,8 @@
 
 def pair_kernel(
     dims,
-    window_ref, text_len_ref, q_ref, k_ref, v_ref, tk_ref, tv_ref, out_ref,
-    keys, values, q_own, q_near, q_far, o_out, o_in, e_out, e_in, held, stats, text_bias,
+    window_hbm, text_len_hbm, q_ref, k_ref, v_ref, tk_ref, tv_ref, out_ref,
+    window_ref, text_len_ref, keys, values, q_own, q_near, q_far, o_out, o_in, e_out, e_in, held, stats, text_bias,
     kv_send, kv_recv, near_send, near_recv, far_send, far_recv, pass_send,
     o_send, o_recv, e_send, e_recv, local_sem,
 ):
@@ -197,6 +197,10 @@
         for i in parts
     ]
     local.append(pltpu.make_async_copy(q_ref, q_own, local_sem.at[4]))
+    scalars = [
+        pltpu.make_async_copy(window_hbm, window_ref, local_sem.at[5]),
+        pltpu.make_async_copy(text_len_hbm, text_len_ref, local_sem.at[6]),
+    ]
 
     def each_head(step):
         def body(h, carry):
@@ -205,30 +209,33 @@
 
         lax.fori_loop(0, heads, body, 0)
 
-    greet(near)
+    def send_kv():
+        for h in range(heads):
+            for i in parts:
+                kv_copy(h, i).start()
 
     @pl.when(inner)
     def _():
         greet(opposite)
-
-    for copy in local:
-        copy.start()
+        greet(near)
+
+    pl.semaphore_wait(barrier, 1)
 
     @pl.when(inner)
     def _():
-        pl.semaphore_wait(barrier, 2)
         for h in range(heads):
             far_copy(h).start()
 
     @pl.when(jnp.logical_not(inner))
     def _():
-        pl.semaphore_wait(barrier, 1)
         for h in range(heads):
             near_copy(h).start()
-
-    for h in range(heads):
-        for i in parts:
-            kv_copy(h, i).start()
+        send_kv()
+
+    for copy in local + scalars:
+        copy.start()
+    for copy in scalars:
+        copy.wait()
 
     index = lax.broadcasted_iota(jnp.int32, text_bias.shape, 0)
     index = index + jnp.where(index < text_tok, me * text_tok, (near - 1) * text_tok)
@@ -255,31 +262,54 @@
             kv_copy(h, i).wait_recv()
         return keys[:, lanes(h)], values[:, lanes(h)].T
 
-    for copy in local:
-        copy.wait()
+    def relay(h):
+        near_copy(h).wait_recv()
+        pass_copy(h).start()
 
     @pl.when(inner)
     def _():
-        for h in range(heads):
-            near_copy(h).wait_recv()
-            pass_copy(h).start()
+        relay(0)
+        send_kv()
+        for h in range(1, heads):
+            relay(h)
+
+        for copy in local:
+            copy.wait()
+
+        def answer(h, j, keys_h, values_t):
+            tile = jnp.where(j == 1, across, opposite)
+            landed = remote(
+                q_near.at[h], q_far.at[h, j], pass_send.at[h], far_recv.at[h, j], opposite
+            )
+            landed.wait_recv()
+            row_max, row_sum, weighted = attend(h, keys_h, values_t, q_far[h, j], tile)
+            o_out[h, j] = (weighted * (1.0 / row_sum)).astype(o_out.dtype)
+            e_out[h, j] = row_max + jnp.log(row_sum) * (1.0 / math.log(2.0))
+            o_copy(h, j, tile).start()
+            e_copy(h, j, tile).start()
 
         def step(h):
             keys_h, values_t = take_kv(h)
-            for j, tile in ((1, across), (0, opposite)):
-                far_recv_copy = pass_copy(h) if j else far_copy(h)
-                far_recv_copy.wait_recv()
-                row_max, row_sum, weighted = attend(h, keys_h, values_t, q_far[h, j], tile)
-                o_out[h, j] = (weighted * (1.0 / row_sum)).astype(o_out.dtype)
-                e_out[h, j] = row_max + jnp.log(row_sum) * (1.0 / math.log(2.0))
-                o_copy(h, j, tile).start()
-                e_copy(h, j, tile).start()
-            hold(h, keys_h, values_t)
+            answer(h, side, keys_h, values_t)
+
+
+            @pl.when(side == 0)
+            def _():
+                hold(h, keys_h, values_t)
+
+            answer(h, 1 - side, keys_h, values_t)
+
+            @pl.when(side == 1)
+            def _():
+                hold(h, keys_h, values_t)
 
         each_head(step)
 
     @pl.when(jnp.logical_not(inner))
     def _():
+        for copy in local:
+            copy.wait()
+
         def step(h):
             hold(h, *take_kv(h))
 
@@ -296,31 +326,44 @@
         result = result + o_in[h].astype(jnp.float32) * (far_part * inverse)
         out_ref[:, lanes(h)] = result.T.astype(out_ref.dtype)
 
-    each_head(finish)
-
-    def sent(h):
-        for i in parts:
-            kv_copy(h, i).wait_send()
-
-    each_head(sent)
+    def waits(copies):
+        for copy in copies:
+            copy.wait_send()
+
+    def kv_sent(h, carry):
+        waits([kv_copy(h, i) for i in parts])
+        return carry
+
+    def finish_to(h, carry):
+        finish(h)
+        return carry
+
+    last = heads - 1
+    lax.fori_loop(0, last, finish_to, 0)
+    lax.fori_loop(0, heads, kv_sent, 0)
 
     @pl.when(inner)
     def _():
-        def done(h):
-            far_copy(h).wait_send()
-            pass_copy(h).wait_send()
-            for j in range(2):
-                o_copy(h, j, across).wait_send()
-                e_copy(h, j, across).wait_send()
-
-        each_head(done)
+        def done(h, carry):
+            waits([far_copy(h), pass_copy(h)])
+            waits([o_copy(h, j, across) for j in range(2)])
+            waits([e_copy(h, j, across) for j in range(2)])
+            return carry
+
+        lax.fori_loop(0, last, done, 0)
+        waits([far_copy(last), pass_copy(last)])
 
     @pl.when(jnp.logical_not(inner))
     def _():
-        def done(h):
+        for h in range(heads):
             near_copy(h).wait_send()
 
-        each_head(done)
+    finish(last)
+
+    @pl.when(inner)
+    def _():
+        waits([o_copy(last, j, across) for j in range(2)])
+        waits([e_copy(last, j, across) for j in range(2)])
 
 
 def assemble_kernel(own_ref, out_ref, sem):
@@ -340,16 +383,17 @@
     grid_cols = min(8, n // 2)
     kind = video_queries.dtype
     any_spec = pl.BlockSpec(memory_space=pl.ANY)
-    smem_spec = pl.BlockSpec(memory_space=pltpu.SMEM)
     key_rows = 2 * (tile_tok + text_tok)
     wide, tall = (tile_tok, head_dim), (head_dim, tile_tok)
     dma = pltpu.SemaphoreType.DMA
     landed = pl.pallas_call(
         functools.partial(pair_kernel, (n, heads, head_dim, grid_cols)),
         out_shape=pltpu.VMEM((tile_tok, features), kind),
-        in_specs=[smem_spec, smem_spec] + [any_spec] * 5,
+        in_specs=[any_spec] * 7,
         out_specs=pl.BlockSpec(memory_space=pltpu.VMEM),
         scratch_shapes=[
+            pltpu.SMEM(head_window.T.shape, head_window.dtype),
+            pltpu.SMEM(text_len.shape, text_len.dtype),
             pltpu.VMEM((key_rows, features), kind),
             pltpu.VMEM((key_rows, features), kind),
             pltpu.VMEM((tile_tok, features), kind),
@@ -364,7 +408,7 @@
             pltpu.VMEM((2 * text_tok, tile_tok), jnp.float32),
             dma((heads, 4)), dma((heads, 4)), dma((heads,)), dma((heads,)),
             dma((heads,)), dma((heads, 2)), dma((heads,)),
-            dma((heads, 2)), dma((heads,)), dma((heads, 2)), dma((heads,)), dma((5,)),
+            dma((heads, 2)), dma((heads,)), dma((heads, 2)), dma((heads,)), dma((7,)),
         ],
         compiler_params=pltpu.CompilerParams(collective_id=0, has_side_effects=True),
         cost_estimate=pl.CostEstimate(

time: 43.4 us -> 42.6 us (0.982)
  Pallas kernels: 42.5 us -> 41.8 us
    pallas_call x1, Pallas kernels: 41.8 us -> 41 us  [paired(): pl.pallas_call(functools.partial(pair_kernel, (n, heads, head_dim, grid_c...]
where the time goes in v2:
time: 42.6 us; the launch traced here: 42.5 us
  Pallas kernels  41.8 us (98%)
  between operations  0.66 us (2%)
    pallas_call x1, Pallas kernels, paired(): pl.pallas_call(functools.partial(pair_kernel, (n, heads, head_dim, grid_c...  41 us

profile of v2, /device:TPU:0, one launch (start us, length us, event | category | flops | bytes accessed | tf_op | source)
XLA Modules:
  0.0 42.5 jit_solution(11231537661698992461)
XLA Ops:
  0.7 41.0 %pair_attend.1.own_ref = bf16[256,768]{1,0:T(8,128)(2,1)S(1)} custom-call(s32[2,6]{1,0:T(2,128)} %bitcast.8, s32[1]{0:T(128)S(6)} %copy.8.text_len_hbm, bf16[256,768]{1,0:T(8,128)(2,1)} %bitcast.5, bf16[256,768]{1,0:T(8,128)(2,1)} %bitcast.6, bf16[256,768]{1,0:T(8,128)(2,1)} %bitcast.7, bf16[64,768]{1,0:T(8,128)(2,1)} %tk_ref.1, bf16[64,768]{1,0:T(8,128)(2,1)} %tv_ref.1), custom_call_target="tpu_custom_call" | custom-call | flops 1509949440 | bytes 6291456 | tf_op jit(solution)/shard_map/pair_attend/pallas_call | solution.py:389
  41.7 0.8 %assemble.1 = bf16[256,768]{1,0:T(8,128)(2,1)} custom-call(bf16[256,768]{1,0:T(8,128)(2,1)S(1)} %pair_attend.1.own_ref), custom_call_target="tpu_custom_call" | custom-call | tf_op jit(solution)/shard_map/assemble/pallas_call | solution.py:429

commit v3 on v1

--- a/solution.py
+++ b/solution.py
@@ -96,22 +96,20 @@
     return result.reshape(slab_count, 1, tile_tok, features).astype(jnp.bfloat16)
 
 
-def partial_attend(keys, values_t, queries, biases, text_bias, log2_scale):
-    tile_tok = queries.shape[0]
+def partial_attend(keys, values_t, queries, blocks, log2_scale):
     scores = lax.dot_general(
         keys, queries, (((1,), (1,)), ((), ())), preferred_element_type=jnp.float32
     )
-    blocks = [scores[i * tile_tok : (i + 1) * tile_tok] for i in range(len(biases))]
-    text = scores[len(biases) * tile_tok :] + text_bias
-    row_max = jnp.max(text, axis=0, keepdims=True)
-    for block, bias in zip(blocks, biases):
-        row_max = jnp.maximum(row_max, jnp.max(block, axis=0, keepdims=True) + bias)
-    row_max = jnp.maximum(row_max, FLOOR)
+    parts, row_max, start = [], jnp.full((1, queries.shape[0]), FLOOR, jnp.float32), 0
+    for length, tile_bias, text_bias in blocks:
+        block = scores[start : start + length]
+        block = block if text_bias is None else block + text_bias
+        row_max = jnp.maximum(row_max, jnp.max(block, axis=0, keepdims=True) + tile_bias)
+        parts.append((block, tile_bias))
+        start += length
     weights = [
-        jnp.exp2(block * log2_scale + (bias - row_max) * log2_scale)
-        for block, bias in zip(blocks, biases)
+        jnp.exp2(block * log2_scale + (bias - row_max) * log2_scale) for block, bias in parts
     ]
-    weights.append(jnp.exp2(text * log2_scale - row_max * log2_scale))
     row_sum = functools.reduce(
         jnp.add, [jnp.sum(weight, axis=0, keepdims=True) for weight in weights]
     )
@@ -122,18 +120,23 @@
 
 def pair_kernel(
     dims,
-    window_ref, text_len_ref, q_ref, k_ref, v_ref, tk_ref, tv_ref, out_ref,
-    keys, values, q_own, q_near, q_far, o_out, o_in, e_out, e_in, held, stats, text_bias,
-    kv_send, kv_recv, near_send, near_recv, far_send, far_recv, pass_send,
-    o_send, o_recv, e_send, e_recv, local_sem,
+    window_hbm, text_len_hbm, q_ref, k_ref, v_ref, tk_ref, tv_ref, out_ref,
+    window_ref, text_len_ref, keys, values, q_own, q_near, q_far,
+    o_out, o_in, e_out, e_in, held, stats, text_bias,
+    bulk_send, query_send, o_send, e_send,
+    kv_recv, near_recv, far_recv, pass_recv, o_recv, e_recv, local_sem,
 ):
     n, heads, head_dim, grid_cols = dims
     tile_tok, text_tok = q_ref.shape[0], tk_ref.shape[0]
     half = n // 2
+    last = heads - 1
     me = lax.axis_index("region")
     side, place = me // half, me % half
     near = side * half + (half - 1 - place)
     inner = side + place == half - 1
+    outer = jnp.logical_not(inner)
+    yields = (side == 1) & (lax.axis_index("head") % 2 == 1)
+    cuts = tuple(min(cut, heads) for cut in (3, 4, 5))
     opposite = n - 1 - me
     across = lax.rem(me + half, n)
     log2_scale = 1.0 / (math.sqrt(head_dim) * math.log(2.0))
@@ -158,37 +161,96 @@
 
     sources = (k_ref, tk_ref, v_ref, tv_ref)
     buffers = (keys, keys, values, values)
-    starts = (0, 2 * tile_tok, 0, 2 * tile_tok)
+    starts = (0, tile_tok, 0, tile_tok)
     lengths = (tile_tok, text_tok, tile_tok, text_tok)
+    side_rows = tile_tok + text_tok
     parts = range(4)
 
     def kv_copy(h, i):
         return remote(
             sources[i].at[:, lanes(h)],
-            buffers[i].at[pl.ds(starts[i] + lengths[i], lengths[i]), lanes(h)],
-            kv_send.at[h, i],
-            kv_recv.at[h, i],
+            buffers[i].at[pl.ds(side_rows + starts[i], lengths[i]), lanes(h)],
+            bulk_send,
+            kv_recv.at[h],
             near,
         )
 
     def near_copy(h):
-        return remote(q_ref.at[:, lanes(h)], q_near.at[h], near_send.at[h], near_recv.at[h], near)
+        return remote(q_ref.at[:, lanes(h)], q_near.at[h], query_send, near_recv.at[h], near)
 
     def far_copy(h):
-        return remote(
-            q_ref.at[:, lanes(h)], q_far.at[h, 0], far_send.at[h], far_recv.at[h, 0], opposite
-        )
+        return remote(q_ref.at[:, lanes(h)], q_far.at[0, h], query_send, far_recv, opposite)
 
     def pass_copy(h):
-        return remote(
-            q_near.at[h], q_far.at[h, 1], pass_send.at[h], far_recv.at[h, 1], opposite
-        )
-
-    def o_copy(h, j, target):
-        return remote(o_out.at[h, j], o_in.at[h], o_send.at[h, j], o_recv.at[h], target)
-
-    def e_copy(h, j, target):
-        return remote(e_out.at[h, j], e_in.at[h], e_send.at[h, j], e_recv.at[h], target)
+        return remote(q_near.at[h], q_far.at[1, h], bulk_send, pass_recv.at[h], opposite)
+
+    def o_copy(h, j, slot, target):
+        return remote(o_out.at[h, j], o_in.at[h, slot], o_send, o_recv.at[h, slot], target)
+
+    def e_copy(h, j, slot, target):
+        return remote(e_out.at[h, j], e_in.at[h, slot], e_send, e_recv.at[h, slot], target)
+
+    def wait_send(ref, sem):
+        remote(ref, ref, sem, far_recv, near).wait_send()
+
+    def some_keys(first, stop):
+        return keys.at[:, pl.ds(first * head_dim, (stop - first) * head_dim)]
+
+    def wait_recv(ref, sem):
+        remote(ref, ref, bulk_send, sem, near).wait_recv()
+
+    def loop(count, step):
+        def body(h, carry):
+            step(h)
+            return carry
+
+        lax.fori_loop(0, count, body, 0)
+
+    def join(h, slots):
+        own_max = stats[h, 0:1, :]
+        top = functools.reduce(jnp.maximum, [e_in[h, slot] for slot in slots], own_max)
+        own_part = jnp.exp2(own_max - top)
+        slot_parts = [jnp.exp2(e_in[h, slot] - top) for slot in slots]
+        inverse = 1.0 / functools.reduce(jnp.add, slot_parts, stats[h, 1:2, :] * own_part)
+        joined = held[h] * (own_part * inverse)
+        for slot, part in zip(slots, slot_parts):
+            joined = joined + o_in[h, slot].astype(jnp.float32) * (part * inverse)
+        out_ref[:, lanes(h)] = joined.T.astype(out_ref.dtype)
+
+    def arrived(h, slot):
+        o_copy(h, 0, slot, near).wait_recv()
+        e_copy(h, 0, slot, near).wait_recv()
+
+    def tile_bias(head, tile_q, tile_k):
+        rows = jnp.abs(tile_q // grid_cols - tile_k // grid_cols)
+        cols = jnp.abs(tile_q % grid_cols - tile_k % grid_cols)
+        within = (rows <= window_ref[0, head]) & (cols <= window_ref[1, head])
+        return jnp.where(within, 0.0, MASKED)
+
+    def key_blocks(h, tile, owners):
+        blocks = []
+        for place, owner in enumerate(owners):
+            blocks.append((tile_tok, tile_bias(h, tile, owner), None))
+            blocks.append((text_tok, 0.0, text_bias[place * text_tok : (place + 1) * text_tok]))
+        return blocks
+
+    def attend(h, rows, tile, owners):
+        used = pl.ds(0, len(owners) * side_rows)
+        keys_h, values_t = keys[used, lanes(h)], values[used, lanes(h)].T
+        return partial_attend(keys_h, values_t, rows, key_blocks(h, tile, owners), log2_scale)
+
+    def hold(h, owners):
+        row_max, row_sum, weighted = attend(h, q_own[:, lanes(h)], me, owners)
+        held[h] = weighted
+        stats[h, 0:1, :] = row_max
+        stats[h, 1:2, :] = row_sum
+
+    def answer(h, j, slot, rows, tile, owners):
+        row_max, row_sum, weighted = attend(h, rows, tile, owners)
+        o_out[h, j] = (weighted * (1.0 / row_sum)).astype(o_out.dtype)
+        e_out[h, j] = row_max + jnp.log(row_sum) * (1.0 / math.log(2.0))
+        o_copy(h, j, slot, tile).start()
+        e_copy(h, j, slot, tile).start()
 
     local = [
         pltpu.make_async_copy(
@@ -197,130 +259,94 @@
         for i in parts
     ]
     local.append(pltpu.make_async_copy(q_ref, q_own, local_sem.at[4]))
-
-    def each_head(step):
-        def body(h, carry):
-            step(h)
-            return carry
-
-        lax.fori_loop(0, heads, body, 0)
-
-    greet(near)
+    local.append(pltpu.make_async_copy(window_hbm, window_ref, local_sem.at[5]))
+    local.append(pltpu.make_async_copy(text_len_hbm, text_len_ref, local_sem.at[6]))
 
     @pl.when(inner)
     def _():
         greet(opposite)
+        greet(near)
+
+    pl.semaphore_wait(barrier, 1)
+
+    @pl.when(inner)
+    def _():
+        for h in range(heads):
+            far_copy(h).start()
+
+    @pl.when(outer)
+    def _():
+        for h in range(heads):
+            near_copy(h).start()
+        first = 0
+        for stop in cuts + (heads,):
+            for h in range(first, stop):
+                for i in parts:
+                    kv_copy(h, i).start()
+            if first < stop < heads:
+
+                @pl.when(yields)
+                def _(first=first, stop=stop):
+                    wait_send(some_keys(first, stop), bulk_send)
+
+            first = stop
 
     for copy in local:
         copy.start()
-
-    @pl.when(inner)
-    def _():
-        pl.semaphore_wait(barrier, 2)
-        for h in range(heads):
-            far_copy(h).start()
-
-    @pl.when(jnp.logical_not(inner))
-    def _():
-        pl.semaphore_wait(barrier, 1)
-        for h in range(heads):
-            near_copy(h).start()
-
-    for h in range(heads):
-        for i in parts:
-            kv_copy(h, i).start()
-
+    for copy in local:
+        copy.wait()
     index = lax.broadcasted_iota(jnp.int32, text_bias.shape, 0)
     index = index + jnp.where(index < text_tok, me * text_tok, (near - 1) * text_tok)
     text_bias[...] = jnp.where(index < text_len_ref[0], 0.0, MASKED)
 
-    def tile_bias(head, tile_q, tile_k):
-        rows = jnp.abs(tile_q // grid_cols - tile_k // grid_cols)
-        cols = jnp.abs(tile_q % grid_cols - tile_k % grid_cols)
-        within = (rows <= window_ref[0, head]) & (cols <= window_ref[1, head])
-        return jnp.where(within, 0.0, MASKED)
-
-    def attend(h, keys_h, values_t, queries, tile):
-        biases = (tile_bias(h, tile, me), tile_bias(h, tile, near))
-        return partial_attend(keys_h, values_t, queries, biases, text_bias[...], log2_scale)
-
-    def hold(h, keys_h, values_t):
-        row_max, row_sum, weighted = attend(h, keys_h, values_t, q_own[:, lanes(h)], me)
-        held[h] = weighted
-        stats[h, 0:1, :] = row_max
-        stats[h, 1:2, :] = row_sum
-
-    def take_kv(h):
-        for i in parts:
-            kv_copy(h, i).wait_recv()
-        return keys[:, lanes(h)], values[:, lanes(h)].T
-
-    for copy in local:
-        copy.wait()
+    @pl.when(outer)
+    def _():
+        loop(heads, lambda h: hold(h, (me,)))
+
+        def finish(h):
+            arrived(h, 1)
+            arrived(h, 0)
+            join(h, (0, 1))
+
+        loop(last, finish)
+        wait_send(q_near, query_send)
+
+        @pl.when(jnp.logical_not(yields))
+        def _():
+            wait_send(some_keys(0, cuts[-1]), bulk_send)
+
+        wait_send(some_keys(cuts[-1], heads), bulk_send)
+        finish(last)
 
     @pl.when(inner)
     def _():
-        for h in range(heads):
+        def relay(h):
             near_copy(h).wait_recv()
             pass_copy(h).start()
+            answer(h, 2, 1, q_near[h], near, (me,))
+
+        loop(heads, relay)
+        wait_recv(q_far.at[0], far_recv)
 
         def step(h):
-            keys_h, values_t = take_kv(h)
-            for j, tile in ((1, across), (0, opposite)):
-                far_recv_copy = pass_copy(h) if j else far_copy(h)
-                far_recv_copy.wait_recv()
-                row_max, row_sum, weighted = attend(h, keys_h, values_t, q_far[h, j], tile)
-                o_out[h, j] = (weighted * (1.0 / row_sum)).astype(o_out.dtype)
-                e_out[h, j] = row_max + jnp.log(row_sum) * (1.0 / math.log(2.0))
-                o_copy(h, j, tile).start()
-                e_copy(h, j, tile).start()
-            hold(h, keys_h, values_t)
-
-        each_head(step)
-
-    @pl.when(jnp.logical_not(inner))
-    def _():
-        def step(h):
-            hold(h, *take_kv(h))
-
-        each_head(step)
-
-    def finish(h):
-        o_copy(h, 0, across).wait_recv()
-        e_copy(h, 0, across).wait_recv()
-        own_max, own_sum, far_max = stats[h, 0:1, :], stats[h, 1:2, :], e_in[h]
-        top = jnp.maximum(own_max, far_max)
-        own_part, far_part = jnp.exp2(own_max - top), jnp.exp2(far_max - top)
-        inverse = 1.0 / (own_sum * own_part + far_part)
-        result = held[h] * (own_part * inverse)
-        result = result + o_in[h].astype(jnp.float32) * (far_part * inverse)
-        out_ref[:, lanes(h)] = result.T.astype(out_ref.dtype)
-
-    each_head(finish)
-
-    def sent(h):
-        for i in parts:
-            kv_copy(h, i).wait_send()
-
-    each_head(sent)
-
-    @pl.when(inner)
-    def _():
-        def done(h):
-            far_copy(h).wait_send()
-            pass_copy(h).wait_send()
-            for j in range(2):
-                o_copy(h, j, across).wait_send()
-                e_copy(h, j, across).wait_send()
-
-        each_head(done)
-
-    @pl.when(jnp.logical_not(inner))
-    def _():
-        def done(h):
-            near_copy(h).wait_send()
-
-        each_head(done)
+            wait_recv(keys.at[:, lanes(h)], kv_recv.at[h])
+            pass_copy(h).wait_recv()
+            answer(h, 1, 0, q_far[1, h], across, (me, near))
+            answer(h, 0, 0, q_far[0, h], opposite, (me, near))
+            hold(h, (me, near))
+
+        loop(heads, step)
+
+        def finish(h):
+            arrived(h, 0)
+            join(h, (0,))
+
+        loop(last, finish)
+        wait_send(q_near, query_send)
+        wait_send(q_near, bulk_send)
+        finish(last)
+        wait_send(o_out, o_send)
+        wait_send(e_out, e_send)
 
 
 def assemble_kernel(own_ref, out_ref, sem):
@@ -340,31 +366,32 @@
     grid_cols = min(8, n // 2)
     kind = video_queries.dtype
     any_spec = pl.BlockSpec(memory_space=pl.ANY)
-    smem_spec = pl.BlockSpec(memory_space=pltpu.SMEM)
     key_rows = 2 * (tile_tok + text_tok)
     wide, tall = (tile_tok, head_dim), (head_dim, tile_tok)
     dma = pltpu.SemaphoreType.DMA
     landed = pl.pallas_call(
         functools.partial(pair_kernel, (n, heads, head_dim, grid_cols)),
         out_shape=pltpu.VMEM((tile_tok, features), kind),
-        in_specs=[smem_spec, smem_spec] + [any_spec] * 5,
+        in_specs=[any_spec] * 7,
         out_specs=pl.BlockSpec(memory_space=pltpu.VMEM),
         scratch_shapes=[
+            pltpu.SMEM(head_window.T.shape, head_window.dtype),
+            pltpu.SMEM(text_len.shape, text_len.dtype),
             pltpu.VMEM((key_rows, features), kind),
             pltpu.VMEM((key_rows, features), kind),
             pltpu.VMEM((tile_tok, features), kind),
             pltpu.VMEM((heads,) + wide, kind),
-            pltpu.VMEM((heads, 2) + wide, kind),
+            pltpu.VMEM((2, heads) + wide, kind),
+            pltpu.VMEM((heads, 3) + tall, kind),
             pltpu.VMEM((heads, 2) + tall, kind),
-            pltpu.VMEM((heads,) + tall, kind),
+            pltpu.VMEM((heads, 3, 1, tile_tok), jnp.float32),
             pltpu.VMEM((heads, 2, 1, tile_tok), jnp.float32),
-            pltpu.VMEM((heads, 1, tile_tok), jnp.float32),
             pltpu.VMEM((heads,) + tall, jnp.float32),
             pltpu.VMEM((heads, 2, tile_tok), jnp.float32),
             pltpu.VMEM((2 * text_tok, tile_tok), jnp.float32),
-            dma((heads, 4)), dma((heads, 4)), dma((heads,)), dma((heads,)),
-            dma((heads,)), dma((heads, 2)), dma((heads,)),
-            dma((heads, 2)), dma((heads,)), dma((heads, 2)), dma((heads,)), dma((5,)),
+            dma, dma, dma, dma,
+            dma((heads,)), dma((heads,)), dma, dma((heads,)),
+            dma((heads, 2)), dma((heads, 2)), dma((7,)),
         ],
         compiler_params=pltpu.CompilerParams(collective_id=0, has_side_effects=True),
         cost_estimate=pl.CostEstimate(

time: 43.4 us -> 40.8 us (0.940)
  the two profiles are of different devices: /device:TPU:0 before, /device:TPU:1 now
where the time goes in v3:
time: 40.8 us; the launch traced here: 40.6 us
  Pallas kernels  39.9 us (98%)
  between operations  0.66 us (2%)
    pallas_call x1, Pallas kernels, paired(): pl.pallas_call(functools.partial(pair_kernel, (n, heads, head_dim, grid_c...  39.2 us

profile of v3, /device:TPU:1, one launch (start us, length us, event | category | flops | bytes accessed | tf_op | source)
XLA Modules:
  0.0 40.6 jit_solution(15404690416368876267)
XLA Ops:
  0.7 39.2 %pair_attend.1.own_ref = bf16[256,768]{1,0:T(8,128)(2,1)S(1)} custom-call(s32[2,6]{1,0:T(2,128)} %bitcast.8, s32[1]{0:T(128)S(6)} %copy.8.text_len_hbm, bf16[256,768]{1,0:T(8,128)(2,1)} %bitcast.5, bf16[256,768]{1,0:T(8,128)(2,1)} %bitcast.6, bf16[256,768]{1,0:T(8,128)(2,1)} %bitcast.7, bf16[64,768]{1,0:T(8,128)(2,1)} %tk_ref.1, bf16[64,768]{1,0:T(8,128)(2,1)} %tv_ref.1), custom_call_target="tpu_custom_call" | custom-call | flops 1509949440 | bytes 6291456 | tf_op jit(solution)/shard_map/pair_attend/pallas_call | solution.py:372
  39.8 0.8 %assemble.1 = bf16[256,768]{1,0:T(8,128)(2,1)} custom-call(bf16[256,768]{1,0:T(8,128)(2,1)S(1)} %pair_attend.1.own_ref), custom_call_target="tpu_custom_call" | custom-call | tf_op jit(solution)/shard_map/assemble/pallas_call | solution.py:412

commit v4 on v3

--- a/solution.py
+++ b/solution.py
@@ -124,19 +124,22 @@
     window_ref, text_len_ref, keys, values, q_own, q_near, q_far,
     o_out, o_in, e_out, e_in, held, stats, text_bias,
     bulk_send, query_send, o_send, e_send,
-    kv_recv, near_recv, far_recv, pass_recv, o_recv, e_recv, local_sem,
+    kv_recv, near_recv, far_recv, pass_recv, o_recv, e_recv, near_o_recv, near_e_recv, local_sem,
 ):
     n, heads, head_dim, grid_cols = dims
     tile_tok, text_tok = q_ref.shape[0], tk_ref.shape[0]
     half = n // 2
     last = heads - 1
+    most_late = min(1, last)
+    late_at = min(5, last)
     me = lax.axis_index("region")
     side, place = me // half, me % half
     near = side * half + (half - 1 - place)
     inner = side + place == half - 1
     outer = jnp.logical_not(inner)
     yields = (side == 1) & (lax.axis_index("head") % 2 == 1)
-    cuts = tuple(min(cut, heads) for cut in (3, 4, 5))
+    late = jnp.where(yields, most_late, 0)
+    cuts = tuple(min(cut, heads) for cut in (1, 2, 3, 4, 5))
     opposite = n - 1 - me
     across = lax.rem(me + half, n)
     log2_scale = 1.0 / (math.sqrt(head_dim) * math.log(2.0))
@@ -184,11 +187,13 @@
     def pass_copy(h):
         return remote(q_near.at[h], q_far.at[1, h], bulk_send, pass_recv.at[h], opposite)
 
-    def o_copy(h, j, slot, target):
-        return remote(o_out.at[h, j], o_in.at[h, slot], o_send, o_recv.at[h, slot], target)
-
-    def e_copy(h, j, slot, target):
-        return remote(e_out.at[h, j], e_in.at[h, slot], e_send, e_recv.at[h, slot], target)
+    def o_copy(h, j, target):
+        landed = near_o_recv if j == 2 else o_recv.at[h]
+        return remote(o_out.at[h, j], o_in.at[j // 2, h], o_send, landed, target)
+
+    def e_copy(h, j, target):
+        landed = near_e_recv if j == 2 else e_recv.at[h]
+        return remote(e_out.at[h, j], e_in.at[j // 2, h], e_send, landed, target)
 
     def wait_send(ref, sem):
         remote(ref, ref, sem, far_recv, near).wait_send()
@@ -206,20 +211,26 @@
 
         lax.fori_loop(0, count, body, 0)
 
+    def late_heads(step):
+        @pl.when(yields)
+        def _():
+            for h in range(heads - most_late, heads):
+                step(h)
+
     def join(h, slots):
         own_max = stats[h, 0:1, :]
-        top = functools.reduce(jnp.maximum, [e_in[h, slot] for slot in slots], own_max)
+        top = functools.reduce(jnp.maximum, [e_in[slot, h] for slot in slots], own_max)
         own_part = jnp.exp2(own_max - top)
-        slot_parts = [jnp.exp2(e_in[h, slot] - top) for slot in slots]
+        slot_parts = [jnp.exp2(e_in[slot, h] - top) for slot in slots]
         inverse = 1.0 / functools.reduce(jnp.add, slot_parts, stats[h, 1:2, :] * own_part)
         joined = held[h] * (own_part * inverse)
         for slot, part in zip(slots, slot_parts):
-            joined = joined + o_in[h, slot].astype(jnp.float32) * (part * inverse)
+            joined = joined + o_in[slot, h].astype(jnp.float32) * (part * inverse)
         out_ref[:, lanes(h)] = joined.T.astype(out_ref.dtype)
 
-    def arrived(h, slot):
-        o_copy(h, 0, slot, near).wait_recv()
-        e_copy(h, 0, slot, near).wait_recv()
+    def arrived(h):
+        o_copy(h, 0, near).wait_recv()
+        e_copy(h, 0, near).wait_recv()
 
     def tile_bias(head, tile_q, tile_k):
         rows = jnp.abs(tile_q // grid_cols - tile_k // grid_cols)
@@ -245,22 +256,22 @@
         stats[h, 0:1, :] = row_max
         stats[h, 1:2, :] = row_sum
 
-    def answer(h, j, slot, rows, tile, owners):
+    def answer(h, j, rows, tile, owners):
         row_max, row_sum, weighted = attend(h, rows, tile, owners)
         o_out[h, j] = (weighted * (1.0 / row_sum)).astype(o_out.dtype)
         e_out[h, j] = row_max + jnp.log(row_sum) * (1.0 / math.log(2.0))
-        o_copy(h, j, slot, tile).start()
-        e_copy(h, j, slot, tile).start()
+        o_copy(h, j, tile).start()
+        e_copy(h, j, tile).start()
 
     local = [
         pltpu.make_async_copy(
-            sources[i], buffers[i].at[pl.ds(starts[i], lengths[i]), :], local_sem.at[i]
+            sources[i], buffers[i].at[pl.ds(starts[i], lengths[i]), :], local_sem.at[0]
         )
         for i in parts
     ]
-    local.append(pltpu.make_async_copy(q_ref, q_own, local_sem.at[4]))
-    local.append(pltpu.make_async_copy(window_hbm, window_ref, local_sem.at[5]))
-    local.append(pltpu.make_async_copy(text_len_hbm, text_len_ref, local_sem.at[6]))
+    local.append(pltpu.make_async_copy(q_ref, q_own, local_sem.at[1]))
+    local.append(pltpu.make_async_copy(window_hbm, window_ref, local_sem.at[2]))
+    local.append(pltpu.make_async_copy(text_len_hbm, text_len_ref, local_sem.at[3]))
 
     @pl.when(inner)
     def _():
@@ -276,11 +287,12 @@
 
     @pl.when(outer)
     def _():
-        for h in range(heads):
-            near_copy(h).start()
+        loop(heads - late, lambda h: near_copy(h).start())
         first = 0
         for stop in cuts + (heads,):
             for h in range(first, stop):
+                if h == late_at:
+                    late_heads(lambda k: near_copy(k).start())
                 for i in parts:
                     kv_copy(h, i).start()
             if first < stop < heads:
@@ -293,7 +305,8 @@
 
     for copy in local:
         copy.start()
-    for copy in local:
+    pltpu.make_async_copy(keys, values, local_sem.at[0]).wait()
+    for copy in local[len(parts) :]:
         copy.wait()
     index = lax.broadcasted_iota(jnp.int32, text_bias.shape, 0)
     index = index + jnp.where(index < text_tok, me * text_tok, (near - 1) * text_tok)
@@ -302,10 +315,11 @@
     @pl.when(outer)
     def _():
         loop(heads, lambda h: hold(h, (me,)))
+        wait_recv(o_in.at[1], near_o_recv)
+        wait_recv(e_in.at[1], near_e_recv)
 
         def finish(h):
-            arrived(h, 1)
-            arrived(h, 0)
+            arrived(h)
             join(h, (0, 1))
 
         loop(last, finish)
@@ -323,22 +337,45 @@
         def relay(h):
             near_copy(h).wait_recv()
             pass_copy(h).start()
-            answer(h, 2, 1, q_near[h], near, (me,))
-
-        loop(heads, relay)
+            answer(h, 2, q_near[h], near, (me,))
+
+        loop(heads - late, relay)
         wait_recv(q_far.at[0], far_recv)
 
         def step(h):
+            @pl.when(h == late_at)
+            def _():
+                late_heads(relay)
+
             wait_recv(keys.at[:, lanes(h)], kv_recv.at[h])
-            pass_copy(h).wait_recv()
-            answer(h, 1, 0, q_far[1, h], across, (me, near))
-            answer(h, 0, 0, q_far[0, h], opposite, (me, near))
+
+            def answer_outer():
+                pass_copy(h).wait_recv()
+                answer(h, 1, q_far[1, h], across, (me, near))
+
+            def answer_inner():
+                answer(h, 0, q_far[0, h], opposite, (me, near))
+
+            @pl.when(side == 1)
+            def _():
+                answer_outer()
+
+                answer_inner()
+
+            @pl.when(side == 0)
+            def _():
+                answer_inner()
+
             hold(h, (me, near))
 
+            @pl.when(side == 0)
+            def _():
+                answer_outer()
+
         loop(heads, step)
 
         def finish(h):
-            arrived(h, 0)
+            arrived(h)
             join(h, (0,))
 
         loop(last, finish)
@@ -383,15 +420,15 @@
             pltpu.VMEM((heads,) + wide, kind),
             pltpu.VMEM((2, heads) + wide, kind),
             pltpu.VMEM((heads, 3) + tall, kind),
-            pltpu.VMEM((heads, 2) + tall, kind),
+            pltpu.VMEM((2, heads) + tall, kind),
             pltpu.VMEM((heads, 3, 1, tile_tok), jnp.float32),
-            pltpu.VMEM((heads, 2, 1, tile_tok), jnp.float32),
+            pltpu.VMEM((2, heads, 1, tile_tok), jnp.float32),
             pltpu.VMEM((heads,) + tall, jnp.float32),
             pltpu.VMEM((heads, 2, tile_tok), jnp.float32),
             pltpu.VMEM((2 * text_tok, tile_tok), jnp.float32),
             dma, dma, dma, dma,
             dma((heads,)), dma((heads,)), dma, dma((heads,)),
-            dma((heads, 2)), dma((heads, 2)), dma((7,)),
+            dma((heads,)), dma((heads,)), dma, dma, dma((4,)),
         ],
         compiler_params=pltpu.CompilerParams(collective_id=0, has_side_effects=True),
         cost_estimate=pl.CostEstimate(

time: 40.8 us -> 40.4 us (level)
  no operation moved by 1% of the time
where the time goes in v4:
time: 40.4 us; the launch traced here: 40.3 us
  Pallas kernels  39.6 us (98%)
  between operations  0.66 us (2%)
    pallas_call x1, Pallas kernels, paired(): pl.pallas_call(functools.partial(pair_kernel, (n, heads, head_dim, grid_c...  38.9 us

profile of v4, /device:TPU:1, one launch (start us, length us, event | category | flops | bytes accessed | tf_op | source)
XLA Modules:
  0.0 40.3 jit_solution(10924184603793840203)
XLA Ops:
  0.7 38.9 %pair_attend.1.own_ref = bf16[256,768]{1,0:T(8,128)(2,1)S(1)} custom-call(s32[2,6]{1,0:T(2,128)} %bitcast.8, s32[1]{0:T(128)S(6)} %copy.8.text_len_hbm, bf16[256,768]{1,0:T(8,128)(2,1)} %bitcast.5, bf16[256,768]{1,0:T(8,128)(2,1)} %bitcast.6, bf16[256,768]{1,0:T(8,128)(2,1)} %bitcast.7, bf16[64,768]{1,0:T(8,128)(2,1)} %tk_ref.1, bf16[64,768]{1,0:T(8,128)(2,1)} %tv_ref.1), custom_call_target="tpu_custom_call" | custom-call | flops 1509949440 | bytes 6291456 | tf_op jit(solution)/shard_map/pair_attend/pallas_call | solution.py:409
  39.5 0.8 %assemble.1 = bf16[256,768]{1,0:T(8,128)(2,1)} custom-call(bf16[256,768]{1,0:T(8,128)(2,1)S(1)} %pair_attend.1.own_ref), custom_call_target="tpu_custom_call" | custom-call | tf_op jit(solution)/shard_map/assemble/pallas_call | solution.py:449

commit v5 on v4

--- a/solution.py
+++ b/solution.py
@@ -188,11 +188,11 @@
         return remote(q_near.at[h], q_far.at[1, h], bulk_send, pass_recv.at[h], opposite)
 
     def o_copy(h, j, target):
-        landed = near_o_recv if j == 2 else o_recv.at[h]
+        landed = near_o_recv if j == 2 else o_recv.at[jnp.where(h == last, 1, 0)]
         return remote(o_out.at[h, j], o_in.at[j // 2, h], o_send, landed, target)
 
     def e_copy(h, j, target):
-        landed = near_e_recv if j == 2 else e_recv.at[h]
+        landed = near_e_recv if j == 2 else e_recv.at[jnp.where(h == last, 1, 0)]
         return remote(e_out.at[h, j], e_in.at[j // 2, h], e_send, landed, target)
 
     def wait_send(ref, sem):
@@ -228,9 +228,10 @@
             joined = joined + o_in[slot, h].astype(jnp.float32) * (part * inverse)
         out_ref[:, lanes(h)] = joined.T.astype(out_ref.dtype)
 
-    def arrived(h):
-        o_copy(h, 0, near).wait_recv()
-        e_copy(h, 0, near).wait_recv()
+    def arrived(group):
+        rows = (pl.ds(0, last), pl.ds(last, 1))[group]
+        wait_recv(o_in.at[0, rows], o_recv.at[group])
+        wait_recv(e_in.at[0, rows], e_recv.at[group])
 
     def tile_bias(head, tile_q, tile_k):
         rows = jnp.abs(tile_q // grid_cols - tile_k // grid_cols)
@@ -240,13 +241,14 @@
 
     def key_blocks(h, tile, owners):
         blocks = []
-        for place, owner in enumerate(owners):
+        for owner in owners:
+            place = 0 if owner is me else 1
             blocks.append((tile_tok, tile_bias(h, tile, owner), None))
             blocks.append((text_tok, 0.0, text_bias[place * text_tok : (place + 1) * text_tok]))
         return blocks
 
     def attend(h, rows, tile, owners):
-        used = pl.ds(0, len(owners) * side_rows)
+        used = pl.ds(0 if owners[0] is me else side_rows, len(owners) * side_rows)
         keys_h, values_t = keys[used, lanes(h)], values[used, lanes(h)].T
         return partial_attend(keys_h, values_t, rows, key_blocks(h, tile, owners), log2_scale)
 
@@ -257,7 +259,15 @@
         stats[h, 1:2, :] = row_sum
 
     def answer(h, j, rows, tile, owners):
-        row_max, row_sum, weighted = attend(h, rows, tile, owners)
+        reply(h, j, tile, *attend(h, rows, tile, owners))
+
+    def merge(first, second):
+        top = jnp.maximum(first[0], second[0])
+        scales = [jnp.exp2(part[0] - top) for part in (first, second)]
+        row_sum = first[1] * scales[0] + second[1] * scales[1]
+        return top, row_sum, first[2] * scales[0] + second[2] * scales[1]
+
+    def reply(h, j, tile, row_max, row_sum, weighted):
         o_out[h, j] = (weighted * (1.0 / row_sum)).astype(o_out.dtype)
         e_out[h, j] = row_max + jnp.log(row_sum) * (1.0 / math.log(2.0))
         o_copy(h, j, tile).start()
@@ -318,11 +328,8 @@
         wait_recv(o_in.at[1], near_o_recv)
         wait_recv(e_in.at[1], near_e_recv)
 
-        def finish(h):
-            arrived(h)
-            join(h, (0, 1))
-
-        loop(last, finish)
+        arrived(0)
+        loop(last, lambda h: join(h, (0, 1)))
         wait_send(q_near, query_send)
 
         @pl.when(jnp.logical_not(yields))
@@ -330,14 +337,21 @@
             wait_send(some_keys(0, cuts[-1]), bulk_send)
 
         wait_send(some_keys(cuts[-1], heads), bulk_send)
-        finish(last)
+        arrived(1)
+        join(last, (0, 1))
 
     @pl.when(inner)
     def _():
-        def relay(h):
+        def relay_only(h):
             near_copy(h).wait_recv()
             pass_copy(h).start()
+
+        def answer_near(h):
             answer(h, 2, q_near[h], near, (me,))
+
+        def relay(h):
+            relay_only(h)
+            answer_near(h)
 
         loop(heads - late, relay)
         wait_recv(q_far.at[0], far_recv)
@@ -345,9 +359,7 @@
         def step(h):
             @pl.when(h == late_at)
             def _():
-                late_heads(relay)
-
-            wait_recv(keys.at[:, lanes(h)], kv_recv.at[h])
+                late_heads(relay_only)
 
             def answer_outer():
                 pass_copy(h).wait_recv()
@@ -358,13 +370,22 @@
 
             @pl.when(side == 1)
             def _():
-                answer_outer()
-
+                pass_copy(h).wait_recv()
+                mine = attend(h, q_far[1, h], across, (me,))
+                wait_recv(keys.at[:, lanes(h)], kv_recv.at[h])
+                theirs = attend(h, q_far[1, h], across, (near,))
+                reply(h, 1, across, *merge(mine, theirs))
                 answer_inner()
 
             @pl.when(side == 0)
             def _():
+                wait_recv(keys.at[:, lanes(h)], kv_recv.at[h])
                 answer_inner()
+
+
+            @pl.when(h == late_at)
+            def _():
+                late_heads(answer_near)
 
             hold(h, (me, near))
 
@@ -374,14 +395,12 @@
 
         loop(heads, step)
 
-        def finish(h):
-            arrived(h)
-            join(h, (0,))
-
-        loop(last, finish)
+        arrived(0)
+        loop(last, lambda h: join(h, (0,)))
         wait_send(q_near, query_send)
         wait_send(q_near, bulk_send)
-        finish(last)
+        arrived(1)
+        join(last, (0,))
         wait_send(o_out, o_send)
         wait_send(e_out, e_send)
 
@@ -428,7 +447,7 @@
             pltpu.VMEM((2 * text_tok, tile_tok), jnp.float32),
             dma, dma, dma, dma,
             dma((heads,)), dma((heads,)), dma, dma((heads,)),
-            dma((heads,)), dma((heads,)), dma, dma, dma((4,)),
+            dma((2,)), dma((2,)), dma, dma, dma((4,)),
         ],
         compiler_params=pltpu.CompilerParams(collective_id=0, has_side_effects=True),
         cost_estimate=pl.CostEstimate(

time: 40.4 us -> 40.2 us (level)
  no operation moved by 1% of the time
where the time goes in v5:
time: 40.2 us; the launch traced here: 40 us
  Pallas kernels  39.4 us (98%)
  between operations  0.66 us (2%)
    pallas_call x1, Pallas kernels, paired(): pl.pallas_call(functools.partial(pair_kernel, (n, heads, head_dim, grid_c...  38.6 us

profile of v5, /device:TPU:1, one launch (start us, length us, event | category | flops | bytes accessed | tf_op | source)
XLA Modules:
  0.0 40.0 jit_solution(4463641792813062489)
XLA Ops:
  0.7 38.6 %pair_attend.1.own_ref = bf16[256,768]{1,0:T(8,128)(2,1)S(1)} custom-call(s32[2,6]{1,0:T(2,128)} %bitcast.8, s32[1]{0:T(128)S(6)} %copy.8.text_len_hbm, bf16[256,768]{1,0:T(8,128)(2,1)} %bitcast.5, bf16[256,768]{1,0:T(8,128)(2,1)} %bitcast.6, bf16[256,768]{1,0:T(8,128)(2,1)} %bitcast.7, bf16[64,768]{1,0:T(8,128)(2,1)} %tk_ref.1, bf16[64,768]{1,0:T(8,128)(2,1)} %tv_ref.1), custom_call_target="tpu_custom_call" | custom-call | flops 1509949440 | bytes 6291456 | tf_op jit(solution)/shard_map/pair_attend/pallas_call | solution.py:428
  39.3 0.8 %assemble.1 = bf16[256,768]{1,0:T(8,128)(2,1)} custom-call(bf16[256,768]{1,0:T(8,128)(2,1)S(1)} %pair_attend.1.own_ref), custom_call_target="tpu_custom_call" | custom-call | tf_op jit(solution)/shard_map/assemble/pallas_call | solution.py:468

commit v6 on v5

--- a/solution.py
+++ b/solution.py
@@ -268,10 +268,10 @@
         return top, row_sum, first[2] * scales[0] + second[2] * scales[1]
 
     def reply(h, j, tile, row_max, row_sum, weighted):
+        e_out[h, j] = row_max + jnp.log(row_sum) * (1.0 / math.log(2.0))
+        e_copy(h, j, tile).start()
         o_out[h, j] = (weighted * (1.0 / row_sum)).astype(o_out.dtype)
-        e_out[h, j] = row_max + jnp.log(row_sum) * (1.0 / math.log(2.0))
         o_copy(h, j, tile).start()
-        e_copy(h, j, tile).start()
 
     local = [
         pltpu.make_async_copy(

time: 40.2 us -> 40.1 us (level)
  no operation moved by 1% of the time
where the time goes in v6:
time: 40.1 us; the launch traced here: 40 us
  Pallas kernels  39.3 us (98%)
  between operations  0.66 us (2%)
    pallas_call x1, Pallas kernels, paired(): pl.pallas_call(functools.partial(pair_kernel, (n, heads, head_dim, grid_c...  38.6 us

profile of v6, /device:TPU:1, one launch (start us, length us, event | category | flops | bytes accessed | tf_op | source)
XLA Modules:
  0.0 40.0 jit_solution(8323706925625360958)
XLA Ops:
  0.7 38.6 %pair_attend.1.own_ref = bf16[256,768]{1,0:T(8,128)(2,1)S(1)} custom-call(s32[2,6]{1,0:T(2,128)} %bitcast.8, s32[1]{0:T(128)S(6)} %copy.8.text_len_hbm, bf16[256,768]{1,0:T(8,128)(2,1)} %bitcast.5, bf16[256,768]{1,0:T(8,128)(2,1)} %bitcast.6, bf16[256,768]{1,0:T(8,128)(2,1)} %bitcast.7, bf16[64,768]{1,0:T(8,128)(2,1)} %tk_ref.1, bf16[64,768]{1,0:T(8,128)(2,1)} %tv_ref.1), custom_call_target="tpu_custom_call" | custom-call | flops 1509949440 | bytes 6291456 | tf_op jit(solution)/shard_map/pair_attend/pallas_call | solution.py:428
  39.2 0.8 %assemble.1 = bf16[256,768]{1,0:T(8,128)(2,1)} custom-call(bf16[256,768]{1,0:T(8,128)(2,1)S(1)} %pair_attend.1.own_ref), custom_call_target="tpu_custom_call" | custom-call | tf_op jit(solution)/shard_map/assemble/pallas_call | solution.py:468

commit v7 on v6

--- a/solution.py
+++ b/solution.py
@@ -138,7 +138,7 @@
     inner = side + place == half - 1
     outer = jnp.logical_not(inner)
     yields = (side == 1) & (lax.axis_index("head") % 2 == 1)
-    late = jnp.where(yields, most_late, 0)
+    late = jnp.where(side == 1, most_late, 0)
     cuts = tuple(min(cut, heads) for cut in (1, 2, 3, 4, 5))
     opposite = n - 1 - me
     across = lax.rem(me + half, n)
@@ -212,7 +212,7 @@
         lax.fori_loop(0, count, body, 0)
 
     def late_heads(step):
-        @pl.when(yields)
+        @pl.when(side == 1)
         def _():
             for h in range(heads - most_late, heads):
                 step(h)
@@ -482,7 +482,7 @@
     slabs, tiles, tile_tok, features = video_queries.shape
     landed = 32 * tile_tok * features
     return (
-        slabs == 1 and tiles == 1 and n // 2 == 2 and n % 2 == 0
+        slabs == 1 and tiles == 1 and heads > 1 and n // 2 == 2 and n % 2 == 0
         and features == 128 * heads and tile_tok % 128 == 0
         and prompt_keys.shape[0] % 16 == 0 and landed < VMEM_BUDGET
     )

time: 40.1 us -> 40.1 us (level)
  no operation moved by 1% of the time
where the time goes in v7:
time: 40.1 us; the launch traced here: 40 us
  Pallas kernels  39.3 us (98%)
  between operations  0.66 us (2%)
    pallas_call x1, Pallas kernels, paired(): pl.pallas_call(functools.partial(pair_kernel, (n, heads, head_dim, grid_c...  38.6 us

profile of v7, /device:TPU:1, one launch (start us, length us, event | category | flops | bytes accessed | tf_op | source)
XLA Modules:
  0.0 40.0 jit_solution(12546089098685686328)
XLA Ops:
  0.7 38.6 %pair_attend.1.own_ref = bf16[256,768]{1,0:T(8,128)(2,1)S(1)} custom-call(s32[2,6]{1,0:T(2,128)} %bitcast.8, s32[1]{0:T(128)S(6)} %copy.8.text_len_hbm, bf16[256,768]{1,0:T(8,128)(2,1)} %bitcast.5, bf16[256,768]{1,0:T(8,128)(2,1)} %bitcast.6, bf16[256,768]{1,0:T(8,128)(2,1)} %bitcast.7, bf16[64,768]{1,0:T(8,128)(2,1)} %tk_ref.1, bf16[64,768]{1,0:T(8,128)(2,1)} %tv_ref.1), custom_call_target="tpu_custom_call" | custom-call | flops 1509949440 | bytes 6291456 | tf_op jit(solution)/shard_map/pair_attend/pallas_call | solution.py:428
  39.2 0.8 %assemble.1 = bf16[256,768]{1,0:T(8,128)(2,1)} custom-call(bf16[256,768]{1,0:T(8,128)(2,1)S(1)} %pair_attend.1.own_ref), custom_call_target="tpu_custom_call" | custom-call | tf_op jit(solution)/shard_map/assemble/pallas_call | solution.py:468

commit v8 on v7

--- a/solution.py
+++ b/solution.py
@@ -139,7 +139,7 @@
     outer = jnp.logical_not(inner)
     yields = (side == 1) & (lax.axis_index("head") % 2 == 1)
     late = jnp.where(side == 1, most_late, 0)
-    cuts = tuple(min(cut, heads) for cut in (1, 2, 3, 4, 5))
+    cuts = tuple(min(cut, heads) for cut in (1, 2, 3, 4))
     opposite = n - 1 - me
     across = lax.rem(me + half, n)
     log2_scale = 1.0 / (math.sqrt(head_dim) * math.log(2.0))

time: 40.1 us -> 40.1 us (level)
  no operation moved by 1% of the time
where the time goes in v8:
time: 40.1 us; the launch traced here: 40 us
  Pallas kernels  39.3 us (98%)
  between operations  0.66 us (2%)
    pallas_call x1, Pallas kernels, paired(): pl.pallas_call(functools.partial(pair_kernel, (n, heads, head_dim, grid_c...  38.6 us

profile of v8, /device:TPU:1, one launch (start us, length us, event | category | flops | bytes accessed | tf_op | source)
XLA Modules:
  0.0 40.0 jit_solution(11002156385456522330)
XLA Ops:
  0.7 38.6 %pair_attend.1.own_ref = bf16[256,768]{1,0:T(8,128)(2,1)S(1)} custom-call(s32[2,6]{1,0:T(2,128)} %bitcast.8, s32[1]{0:T(128)S(6)} %copy.8.text_len_hbm, bf16[256,768]{1,0:T(8,128)(2,1)} %bitcast.5, bf16[256,768]{1,0:T(8,128)(2,1)} %bitcast.6, bf16[256,768]{1,0:T(8,128)(2,1)} %bitcast.7, bf16[64,768]{1,0:T(8,128)(2,1)} %tk_ref.1, bf16[64,768]{1,0:T(8,128)(2,1)} %tv_ref.1), custom_call_target="tpu_custom_call" | custom-call | flops 1509949440 | bytes 6291456 | tf_op jit(solution)/shard_map/pair_attend/pallas_call | solution.py:428
  39.2 0.8 %assemble.1 = bf16[256,768]{1,0:T(8,128)(2,1)} custom-call(bf16[256,768]{1,0:T(8,128)(2,1)S(1)} %pair_attend.1.own_ref), custom_call_target="tpu_custom_call" | custom-call | tf_op jit(solution)/shard_map/assemble/pallas_call | solution.py:468

commit v9 on v6

--- a/solution.py
+++ b/solution.py
@@ -403,12 +403,6 @@
         join(last, (0,))
         wait_send(o_out, o_send)
         wait_send(e_out, e_send)
-
-
-def assemble_kernel(own_ref, out_ref, sem):
-    copy = pltpu.make_async_copy(own_ref, out_ref, sem)
-    copy.start()
-    copy.wait()
 
 
 def paired(
@@ -465,15 +459,7 @@
         prompt_keys,
         prompt_values,
     )
-    result = pl.pallas_call(
-        assemble_kernel,
-        out_shape=jax.ShapeDtypeStruct((tile_tok, features), kind),
-        in_specs=[pl.BlockSpec(memory_space=pltpu.VMEM)],
-        out_specs=any_spec,
-        scratch_shapes=[dma],
-        name="assemble",
-    )(pltpu.with_memory_space_constraint(landed, pltpu.VMEM))
-    return result.reshape(video_queries.shape)
+    return landed.reshape(video_queries.shape)
 
 
 def fits(video_queries, head_window, prompt_keys):

time: 40.1 us -> 40.1 us (level)
  local copies, waits for them, and re-layouts: 0 us -> 0.75 us
  Pallas kernels: 39.3 us -> 38.6 us
    pallas_call x1 -> x0, Pallas kernels: 0.76 us -> none  [paired(): pl.pallas_call(assemble_kernel, out_shape=jax.ShapeDtypeStruct((tile_tok,...]
    unnamed x0 -> x1, local copies, waits for them, and re-layouts: none -> 0.75 us
where the time goes in v9:
time: 40.1 us; the launch traced here: 40 us
  Pallas kernels  38.6 us (96%)
  local copies, waits for them, and re-layouts  0.75 us (2%)
  between operations  0.66 us (2%)
    pallas_call x1, Pallas kernels, paired(): pl.pallas_call(functools.partial(pair_kernel, (n, heads, head_dim, grid_c...  38.6 us

profile of v9, /device:TPU:1, one launch (start us, length us, event | category | flops | bytes accessed | tf_op | source)
XLA Modules:
  0.0 40.0 jit_solution(5335605804564262181)
XLA Ops:
  0.7 38.6 %pair_attend.1 = bf16[256,768]{1,0:T(8,128)(2,1)S(1)} custom-call(s32[2,6]{1,0:T(2,128)} %bitcast.9, s32[1]{0:T(128)S(6)} %copy.10.text_len_hbm, bf16[256,768]{1,0:T(8,128)(2,1)} %bitcast.6, bf16[256,768]{1,0:T(8,128)(2,1)} %bitcast.7, bf16[256,768]{1,0:T(8,128)(2,1)} %bitcast.8, bf16[64,768]{1,0:T(8,128)(2,1)} %tk_ref.1, bf16[64,768]{1,0:T(8,128)(2,1)} %tv_ref.1), custom_call_target="tpu_custom_call" | custom-call | flops 1509949440 | bytes 6291456 | tf_op jit(solution)/shard_map/pair_attend/pallas_call | solution.py:422
  39.2 0.7 %copy.9 = bf16[1,1,256,768]{3,2,1,0:T(8,128)(2,1)} copy(bf16[1,1,256,768]{3,2,1,0:T(8,128)(2,1)S(1)} %bitcast.5) | data formatting | bytes 786432

commit v10 on v6

--- a/solution.py
+++ b/solution.py
@@ -226,7 +226,7 @@
         joined = held[h] * (own_part * inverse)
         for slot, part in zip(slots, slot_parts):
             joined = joined + o_in[slot, h].astype(jnp.float32) * (part * inverse)
-        out_ref[:, lanes(h)] = joined.T.astype(out_ref.dtype)
+        out_ref[:, lanes(h)] = joined.astype(out_ref.dtype).T
 
     def arrived(group):
         rows = (pl.ds(0, last), pl.ds(last, 1))[group]

time: 40.1 us -> 40.1 us (level)
  no operation moved by 1% of the time
where the time goes in v10:
time: 40.1 us; the launch traced here: 40 us
  Pallas kernels  39.3 us (98%)
  between operations  0.66 us (2%)
    pallas_call x1, Pallas kernels, paired(): pl.pallas_call(functools.partial(pair_kernel, (n, heads, head_dim, grid_c...  38.5 us

profile of v10, /device:TPU:1, one launch (start us, length us, event | category | flops | bytes accessed | tf_op | source)
XLA Modules:
  0.0 40.0 jit_solution(7267355620578670649)
XLA Ops:
  0.7 38.5 %pair_attend.1.own_ref = bf16[256,768]{1,0:T(8,128)(2,1)S(1)} custom-call(s32[2,6]{1,0:T(2,128)} %bitcast.8, s32[1]{0:T(128)S(6)} %copy.8.text_len_hbm, bf16[256,768]{1,0:T(8,128)(2,1)} %bitcast.5, bf16[256,768]{1,0:T(8,128)(2,1)} %bitcast.6, bf16[256,768]{1,0:T(8,128)(2,1)} %bitcast.7, bf16[64,768]{1,0:T(8,128)(2,1)} %tk_ref.1, bf16[64,768]{1,0:T(8,128)(2,1)} %tv_ref.1), custom_call_target="tpu_custom_call" | custom-call | flops 1509949440 | bytes 6291456 | tf_op jit(solution)/shard_map/pair_attend/pallas_call | solution.py:428
  39.2 0.8 %assemble.1 = bf16[256,768]{1,0:T(8,128)(2,1)} custom-call(bf16[256,768]{1,0:T(8,128)(2,1)S(1)} %pair_attend.1.own_ref), custom_call_target="tpu_custom_call" | custom-call | tf_op jit(solution)/shard_map/assemble/pallas_call | solution.py:468
